TPU v7x, 32 devices: a whole 2x2x4 slice. The times are simulated.
32 devices in a mesh: blocks: 8 (over z, x), span: 4 (over y, core).
Axes of the slice: x: 2, y: 2, z: 4, core: 2. Of those that a mesh axis runs over, the one named last changes fastest.
Arguments:
- struct_disp: float32 [3, 16384], P(None, ('blocks', 'span')), may hold values from -3 to 3
- rec_struct: int32 [16384], P(('blocks', 'span')), may hold values from 0 to 511
- rec_block: int32 [16384, 1], P(('blocks', 'span')), may hold values from 0 to 7; in each aligned block of 512 rows (0 to 511, 512 to 1023, ...) at most 128 rows name the same one
- rec_node: int32 [16384], P(('blocks', 'span')), may hold values from 0 to 8191
- rec_weight: float32 [16384], P(('blocks', 'span')), may hold values from 0.2 to 1
- offset: float32 [3, 16, 256, 1024], P(None, None, 'blocks', 'span'), may hold values from -0.6 to 0.6
- prior_warp: float32 [3, 16, 256, 1024], P(None, None, 'blocks', 'span'), may hold values from -3 to 3
- inv_volume: float32 [16, 256, 1024], P(None, 'blocks', 'span'), may hold values from 0.04 to 0.16
- coord_cot: float32 [3, 16, 256, 1024], P(None, None, 'blocks', 'span'), may hold values from -6 to 6
- vol_cot: float32 [16, 256, 1024], P(None, 'blocks', 'span'), may hold values from -6 to 6
Outputs:
- warp_field: float32 [3, 16, 256, 1024], P(None, None, 'blocks', 'span')
- mesh_adjoint: float32 [3, 16, 256, 1024], P(None, None, 'blocks', 'span')
- struct_sens: float32 [3, 16384], P(None, ('blocks', 'span'))
Inputs may be any that keep to these rules, and one draw needn't show every extreme that they name: `rec_block`: in the rows of one device no fluid group is named by more than 128 records, and on some devices one group is named by exactly 128.
All inputs are finite; a program needn't handle non-finite values.
Results may differ from a plain program's by a relative error of at most 0.00002.
Values sent between devices are 32-bit elements; how exact they have to be, the bound alone decides.
A program may use at most 128 MiB of HBM per device.

v0:
```python
import functools

import jax
import jax.numpy as jnp
from jax import lax
from jax.experimental import pallas as pl
from jax.experimental.pallas import tpu as pltpu
from jax.sharding import PartitionSpec as P

SWEEPS = 4
LANES = 128
SUB = 8
VMEM_LIMIT = 62 * 1024 * 1024
MESH = pl.DeviceIdType.MESH


def split3(x):
    hi = x.astype(jnp.bfloat16)
    rest = x - hi.astype(jnp.float32)
    mid = rest.astype(jnp.bfloat16)
    low = (rest - mid.astype(jnp.float32)).astype(jnp.bfloat16)
    return hi, mid, low


def iota(shape, dim):
    return lax.broadcasted_iota(jnp.int32, shape, dim)


def kernel(
    groups,
    slabs,
    struct_of,
    block_of,
    node_of,
    weight_of,
    disp,
    offset_h,
    prior_h,
    inv_h,
    cot_h,
    vol_h,
    warp_h,
    adj_o,
    sens_o,
    va,
    vb,
    sb,
    low_i,
    low_j,
    rec_send,
    rec_got,
    reply_send,
    reply_got,
    ja_send,
    ja_got,
    ka_send,
    ka_got,
    surf_got,
    jb_send,
    jb_got,
    kb_send,
    kb_got,
    jc_send,
    jc_got,
    kc_send,
    kc_got,
    sem_rec,
    sem_reply,
    sem_halo,
    cot,
    sem_in,
    sem_out,
):
    ni, nj, nk = offset_h.shape[1:]
    half = ni // 2
    np_j = nj + SUB
    tiles = nk // LANES
    own, top, end = slice(SUB, SUB + nj), slice(0, SUB), slice(SUB + nj, SUB + nj + SUB)
    near = SUB - SWEEPS
    lanes_of = lambda t: slice(t * LANES, (t + 1) * LANES)
    records = struct_of.shape[0]
    f32, bf16 = jnp.float32, jnp.bfloat16
    me = lax.axis_index("blocks")
    my = lax.axis_index("span")
    has = (me > 0, me < groups - 1, my > 0, my < slabs - 1)
    where_to = ((me - 1, my), (me + 1, my), (me, my - 1), (me, my + 1))

    def load(number, src, dst):
        copies = []
        for t in range(tiles):
            lanes = slice(t * LANES, (t + 1) * LANES)
            copies.append(
                pltpu.make_async_copy(src(lanes), dst(t), sem_in.at[number, t])
            )
            copies[-1].start()
        return copies

    load_prior = load(0, lambda x: prior_h.at[:, :, :, x], lambda t: va.at[0:3, :, t, own, :])
    load_inv = load(1, lambda x: inv_h.at[:, :, x], lambda t: va.at[3, :, t, own, :])
    load_offset = load(2, lambda x: offset_h.at[:, :, :, x], lambda t: sb.at[0:3, :, t, own, :])
    load_vol = load(3, lambda x: vol_h.at[:, :, x], lambda t: sb.at[3, :, t, own, :])
    load_cot = load(4, lambda x: cot_h.at[:, :, :, x], lambda t: cot.at[:, :, :, lanes_of(t)])

    def arrived(copies):
        for copy in copies:
            copy.wait()

    barrier = pltpu.get_barrier_semaphore()
    for step in range(1, groups):
        pl.semaphore_signal(
            barrier, inc=1, device_id=(lax.rem(me + step, groups), my), device_id_type=MESH
        )
    for side in (2, 3):

        @pl.when(has[side])
        def _(side=side):
            pl.semaphore_signal(barrier, inc=1, device_id=where_to[side], device_id_type=MESH)

    def flat(ref):
        return ref[...].reshape(1, records)

    weights = flat(weight_of)
    node = flat(node_of)
    row_in = node // nk
    onehot_s = (iota((disp.shape[1], records), 0) == flat(struct_of)).astype(bf16)
    parts = jnp.concatenate(split3(disp[...]), axis=0)
    gathered = jnp.dot(parts, onehot_s, preferred_element_type=f32)
    rec_send[0:3, :] = (gathered[0:3] + gathered[3:6] + gathered[6:9]) * weights
    rec_send[3:4, :] = (flat(block_of) * nj + row_in).astype(f32)
    rec_send[4:5, :] = (node - row_in * nk).astype(f32)
    rec_send[5:8, :] = jnp.zeros((3, records), f32)

    pl.semaphore_wait(
        barrier, groups - 1 + has[2].astype(jnp.int32) + has[3].astype(jnp.int32)
    )

    def rec_copy(step):
        return pltpu.make_async_remote_copy(
            src_ref=rec_send,
            dst_ref=rec_got.at[me],
            send_sem=sem_rec.at[0, step],
            recv_sem=sem_rec.at[1, step],
            device_id=(lax.rem(me + step, groups), my),
            device_id_type=MESH,
        )

    for step in range(1, groups):
        rec_copy(step).start()
    rec_got[me] = rec_send[...]

    def move(side, src, dst, number):
        return pltpu.make_async_remote_copy(
            src_ref=src,
            dst_ref=dst,
            send_sem=sem_halo.at[0, number, side],
            recv_sem=sem_halo.at[1, number, side],
            device_id=where_to[side],
            device_id_type=MESH,
        )

    def start(side, src, dst, number):
        @pl.when(has[side])
        def _():
            move(side, src, dst, number).start()

    def finish_recv(side, src, dst, number):
        @pl.when(has[side ^ 1])
        def _():
            move(side, src, dst, number).wait_recv()

    def finish_send(side, src, dst, number):
        @pl.when(has[side])
        def _():
            move(side, src, dst, number).wait_send()

    def clear_missing(side, ref):
        @pl.when(jnp.logical_not(has[side ^ 1]))
        def _():
            ref[...] = jnp.zeros(ref.shape, f32)

    row8 = iota((SUB, nk), 0)
    lane_nj = iota((nj, LANES), 1)
    rows_k = nj + 2 * SUB
    lane_np = iota((rows_k, LANES), 1)

    def pack_rows4(source, send, comps):
        for c in range(comps):

            @pl.loop(0, half)
            def _(i):
                a, b = source(c, i, 0), source(c, i + half, 0)
                send[0, c, i] = jnp.where(row8 < SWEEPS, a, pltpu.roll(b, SWEEPS, 0))
                a, b = source(c, i, nj - SUB), source(c, i + half, nj - SUB)
                send[1, c, i] = jnp.where(row8 < SWEEPS, pltpu.roll(b, SWEEPS, 0), a)

    def put(target, c, i, rows, value):
        for t in range(tiles):
            target[c, i, t, rows, :] = value[:, t * LANES : (t + 1) * LANES]

    def unpack_rows4(got, comps, store):
        for c in range(comps):

            @pl.loop(0, half)
            def _(i):
                for side, rows in ((0, end), (1, top)):
                    x = got[side, c, i]
                    store(c, i, rows, x)
                    store(c, i + half, rows, pltpu.roll(x, SWEEPS, 0))

    def pack_lanes(source, send, comps, width):
        per = LANES // width
        total = comps * ni
        chunk = lane_nj // width
        for g in range(-(-total // per)):

            def step(p, kept, g=g):
                first, last = kept
                s = g * per + p
                c, i = s // ni, s % ni
                left = source[c, i, 0, own, :]
                right = source[c, i, tiles - 1, own, :]
                both = pltpu.roll(
                    jnp.where(lane_nj < LANES // 2, left, right), p * width, 1
                )
                first = jnp.where(chunk == p, both, first)
                last = jnp.where(chunk == lax.rem(p + per - 1, per), both, last)
                return first, last

            zero = jnp.zeros((nj, LANES), f32)
            first, last = lax.fori_loop(
                0, min(per, total - g * per), step, (zero, zero), unroll=4
            )
            send[0, g] = first
            send[1, g] = last

    def unpack_lanes(got, target, comps, width):
        per = LANES // width
        total = comps * ni
        chunk = lane_np // width
        for g in range(-(-total // per)):
            after, before = got[0, g], got[1, g]

            def step(p, kept, g=g, after=after, before=before):
                s = g * per + p
                c, i = s // ni, s % ni
                both = jnp.where(chunk == p, after, before)
                target[c, i, tiles] = pltpu.roll(both, lax.rem(LANES - p * width, LANES), 1)
                return kept

            lax.fori_loop(0, min(per, total - g * per), step, 0, unroll=4)

    class Exchange:
        def __init__(self, number, j_send, j_got, k_send, k_got):
            self.j = [(j_send.at[s], j_got.at[s], number) for s in (0, 1)]
            self.k = [(k_send.at[s], k_got.at[s, :, own, :], number) for s in (0, 1)]
            self.c = []
            for s in (0, 1):
                at = SUB + s * (nj - SUB)
                to = (end, top)[s]
                self.c.append(
                    (k_got.at[:, :, at : at + SUB, :], k_got.at[:, :, to, :], number + 1)
                )
                clear_missing(s, j_got.at[s])
                clear_missing(2 + s, k_got.at[s, :, own, :])
                clear_missing(s, k_got.at[:, :, to, :])

        def start_j(self):
            for s in (0, 1):
                start(s, *self.j[s])

        def start_k(self):
            for s in (0, 1):
                start(2 + s, *self.k[s])

        def corners(self):
            for s in (0, 1):
                finish_recv(2 + s, *self.k[s])
            for s in (0, 1):
                start(s, *self.c[s])

        def finish(self):
            for s in (0, 1):
                finish_recv(s, *self.j[s])
                finish_recv(s, *self.c[s])

        def sent(self):
            for s in (0, 1):
                finish_send(s, *self.j[s])
                finish_send(2 + s, *self.k[s])
                finish_send(s, *self.c[s])

    halo_a = Exchange(0, ja_send, ja_got, ka_send, ka_got)

    def source(c, i, at):
        rows = slice(SUB + at, 2 * SUB + at)
        return jnp.concatenate([va[c, i, t, rows, :] for t in range(tiles)], axis=1)

    arrived(load_prior)
    arrived(load_inv)
    pack_rows4(source, ja_send, 4)
    halo_a.start_j()

    pack_lanes(va, ka_send, 4, SWEEPS)
    halo_a.start_k()

    row_p = iota((np_j, records), 0)
    row_of = (me * nj + row_p - SWEEPS).astype(f32)
    col_of = iota((nk, records), 0).astype(f32)

    def scatter(g, total):
        got = rec_got[g]
        here = row_of == got[3:4, :]
        cols = (col_of == got[4:5, :]).astype(bf16)
        pieces = split3(got[0:3, :])
        left = jnp.concatenate(
            [
                jnp.where(here, pieces[n][c : c + 1, :].astype(f32), 0.0)
                for n in range(3)
                for c in range(3)
            ],
            axis=0,
        ).astype(bf16)
        out = lax.dot_general(
            left, cols, (((1,), (1,)), ((), ())), preferred_element_type=f32
        )
        rows = 3 * np_j
        return total + (out[0:rows] + out[rows : 2 * rows] + out[2 * rows :])

    def scatter_next(step, total):
        rec_copy(step).wait_recv()
        return scatter(lax.rem(me - step + groups, groups), total)

    surface = scatter(me, jnp.zeros((3 * np_j, nk), f32))
    surface = lax.fori_loop(1, groups, scatter_next, surface)
    for c in range(3):
        put(va, c, 0, slice(near, near + np_j), surface[c * np_j : (c + 1) * np_j])

    halo_a.corners()
    surf = [
        (va.at[0:3, 0, s * (tiles - 1)], surf_got.at[s], 6)
        for s in (0, 1)
    ]
    for s in (0, 1):
        clear_missing(2 + s, surf_got.at[s])
        start(2 + s, *surf[s])
    halo_a.finish()

    def store_a(c, i, rows, value):
        if c < 3:

            @pl.when(i > 0)
            def _():
                put(va, c, i, rows, value)
        else:
            put(va, c, i, rows, value)

    unpack_rows4(ja_got, 4, store_a)
    unpack_lanes(ka_got, va, 4, SWEEPS)
    for s in (0, 1):
        finish_recv(2 + s, *surf[s])
    for c in range(3):
        va[c, 0, tiles] = jnp.where(lane_np < LANES // 2, surf_got[0, c], surf_got[1, c])
    halo_a.sent()
    for s in (0, 1):
        finish_send(2 + s, *surf[s])

    for c in range(3):
        vb[c, 0] = va[c, 0]
        vb[c, ni - 1] = va[c, ni - 1]

    def nearby(rows):
        return slice(rows.start - 1, rows.stop - 1), slice(rows.start + 1, rows.stop + 1)

    def lane_before(x, rolled):
        lane = iota(x[0].shape, 1)
        return [jnp.where(lane == 0, rolled[t - 1], rolled[t]) for t in range(len(x))]

    def lane_after(x, rolled):
        lane = iota(x[0].shape, 1)
        count = len(x)
        return [
            jnp.where(lane == LANES - 1, rolled[(t + 1) % count], rolled[t])
            for t in range(count)
        ]

    def changes(src, c, i, rows, count):
        low, high = nearby(rows)
        x = [src[c, i, t, rows, :] for t in range(tiles + 1)]
        before = lane_before(x, [pltpu.roll(v, 1, 1) for v in x])
        after = lane_after(x, [pltpu.roll(v, LANES - 1, 1) for v in x])
        out = []
        for t in range(count):
            total = before[t] + after[t]
            total = total + (src[c, i, t, low, :] + src[c, i, t, high, :])
            total = total + (src[c, i - 1, t, rows, :] + src[c, i + 1, t, rows, :])
            out.append(total - 6.0 * x[t])
        return x, out

    wide = slice(near, near + np_j)

    def in_pairs(first, stop):
        def run(step):
            even = first + (stop - first) // 2 * 2
            if even > first:
                pl.loop(first, even, unroll=2)(step)
            if even < stop:
                step(even)

        return run

    def sweep_a(src, dst, last):
        rows, count = (own, tiles) if last else (wide, tiles + 1)

        @in_pairs(1, ni - 1)
        def _(i):
            for c in range(3):
                x, change = changes(src, c, i, rows, count)
                for t in range(count):
                    dst[c, i, t, rows, :] = x[t] + va[3, i, t, rows, :] * change[t]

    for sweep in range(SWEEPS):
        src, dst = (va, vb) if sweep % 2 == 0 else (vb, va)
        sweep_a(src, dst, sweep == SWEEPS - 1)

    done = va if SWEEPS % 2 == 0 else vb

    halo_b = Exchange(2, jb_send, jb_got, kb_send, kb_got)

    warp_out = []
    for t in range(tiles):
        warp_out.append(
            pltpu.make_async_copy(
                done.at[0:3, :, t, own, :], warp_h.at[:, :, :, lanes_of(t)], sem_out.at[t]
            )
        )
        warp_out[-1].start()
    arrived(load_offset)
    arrived(load_vol)

    @pl.loop(0, ni)
    def _(i):
        for c in range(4):
            for t in range(tiles):
                value = sb[c, i, t, own, :]
                if c < 3:
                    value = value + done[c, i, t, own, :]
                    sb[c, i, t, own, :] = value
                jb_send[0, c, t, pl.ds(i, 1), :] = value[0:1]
                jb_send[1, c, t, pl.ds(i, 1), :] = value[nj - 1 : nj]

    halo_b.start_j()
    pack_lanes(sb, kb_send, 4, 1)
    halo_b.start_k()
    halo_b.corners()
    halo_b.finish()

    @pl.loop(0, ni)
    def _(i):
        for c in range(4):
            for side, rows in ((0, end), (1, top)):
                for t in range(tiles):
                    sb[c, i, t, rows, :] = jnp.broadcast_to(
                        jb_got[side, c, t, pl.ds(i, 1), :], (SUB, LANES)
                    )

    unpack_lanes(kb_got, sb, 4, 1)
    halo_b.sent()

    lane = iota((np_j, LANES), 1)
    row_at = me * nj + iota((np_j, LANES), 0) - SWEEPS
    row_in = (row_at >= 0) & (row_at < groups * nj - 1)

    def inside(t):
        if t < tiles:
            at = my * nk + t * LANES + lane
        else:
            at = my * nk + lane - LANES
        return row_in & (at >= 0) & (at < slabs * nk - 1)

    def cross(a, b):
        return (
            a[1] * b[2] - a[2] * b[1],
            a[2] * b[0] - a[0] * b[2],
            a[0] * b[1] - a[1] * b[0],
        )

    low_i[...] = jnp.zeros(low_i.shape, f32)
    arrived(load_cot)
    arrived(warp_out)
    mine = slice(SWEEPS, SWEEPS + nj)
    _, wide_high = nearby(wide)

    @pl.loop(0, ni)
    def _(i):
        above = jnp.minimum(i + 1, ni - 1)
        held = None
        for t in (tiles, *range(tiles)):
            follow = (t + 1) % (tiles + 1)
            base = [sb[c, i, t, wide, :] for c in range(3)]
            edge_i = [sb[c, above, t, wide, :] - base[c] for c in range(3)]
            edge_j = [sb[c, i, t, wide_high, :] - base[c] for c in range(3)]
            edge_k = [
                jnp.where(
                    lane == LANES - 1,
                    pltpu.roll(sb[c, i, follow, wide, :], LANES - 1, 1),
                    pltpu.roll(base[c], LANES - 1, 1),
                )
                - base[c]
                for c in range(3)
            ]
            edge_i[0] = edge_i[0] + 1.0
            edge_j[1] = edge_j[1] + 1.0
            edge_k[2] = edge_k[2] + 1.0
            weight = jnp.where(inside(t) & (i < ni - 1), sb[3, i, t, wide, :], 0.0)
            grad_k = [pltpu.roll(weight * g, 1, 1) for g in cross(edge_i, edge_j)]
            if t < tiles:
                grad_i = cross(edge_j, edge_k)
                grad_j = cross(edge_k, edge_i)
                rate = va[3, i, t, own, :]
                rate = jnp.where((i > 0) & (i < ni - 1), rate, 0.0)
                for c in range(3):
                    gi = (weight * grad_i[c])[mine]
                    low_j[c, t] = weight * grad_j[c]
                    gk = weight * cross(edge_i, edge_j)[c]
                    rest = jnp.where(lane == 0, held[c], grad_k[c]) - gk
                    rest = rest[mine] + (
                        low_j[c, t, SWEEPS - 1 : SWEEPS - 1 + nj, :] - low_j[c, t, mine, :]
                    )
                    lanes = slice(t * LANES, (t + 1) * LANES)
                    out = cot[c, i, :, lanes] - gi + low_i[c, t] + rest
                    low_i[c, t] = gi
                    adj_o[c, i, :, lanes] = out
                    va[c, i, t, own, :] = rate * out
            held = grad_k

    halo_c = Exchange(4, jc_send, jc_got, kc_send, kc_got)

    pack_rows4(source, jc_send, 3)
    halo_c.start_j()
    pack_lanes(va, kc_send, 3, SWEEPS)
    halo_c.start_k()
    halo_c.corners()
    halo_c.finish()

    def store_c(c, i, rows, value):
        put(va, c, i, rows, value)

    unpack_rows4(jc_got, 3, store_c)
    unpack_lanes(kc_got, va, 3, SWEEPS)
    halo_c.sent()
    for c in range(3):
        vb[c, 0] = jnp.zeros(vb.shape[2:], f32)
        vb[c, ni - 1] = jnp.zeros(vb.shape[2:], f32)

    def sweep_c(sweep, first, stop):
        src, dst = (va, vb) if sweep % 2 == 0 else (vb, va)
        last = sweep == SWEEPS - 1
        rows, count = (own, tiles) if last else (wide, tiles + 1)
        kept = slice(0, nj) if last else mine

        @in_pairs(first, stop)
        def _(i):
            for c in range(3):
                x, change = changes(src, c, i, rows, count)
                for t in range(count):
                    if t < tiles:
                        adj_o[c, i, :, t * LANES : (t + 1) * LANES] += change[t][kept]
                    if not last:
                        dst[c, i, t, rows, :] = x[t] + va[3, i, t, rows, :] * change[t]

    def add_wall(sweep, wall, layer):
        src = va if sweep % 2 == 0 else vb
        for c in range(3):
            for t in range(tiles):
                adj_o[c, wall, :, t * LANES : (t + 1) * LANES] += src[c, layer, t, own, :]

    add_wall(0, 0, 1)
    for sweep in range(SWEEPS - 1):
        sweep_c(sweep, 1, SWEEPS - sweep)
        add_wall(sweep + 1, 0, 1)

    wall = jnp.concatenate(
        [jnp.concatenate(split3(adj_o[c, 0]), axis=0) for c in range(3)], axis=0
    )
    row_w = (me * nj + iota((nj, records), 0)).astype(f32)

    def reply_copy(step):
        to = lax.rem(me + step, groups)
        return pltpu.make_async_remote_copy(
            src_ref=reply_send.at[to],
            dst_ref=reply_got.at[me],
            send_sem=sem_reply.at[0, step],
            recv_sem=sem_reply.at[1, step],
            device_id=(to, my),
            device_id_type=MESH,
        )

    def answer(g):
        got = rec_got[g]
        cols = (col_of == got[4:5, :]).astype(bf16)
        here = row_w == got[3:4, :]
        out = jnp.dot(wall, cols, preferred_element_type=f32)
        for c in range(3):
            at = 3 * c * nj
            value = (
                out[at : at + nj] + out[at + nj : at + 2 * nj] + out[at + 2 * nj : at + 3 * nj]
            )
            reply_send[g, c : c + 1, :] = jnp.sum(
                jnp.where(here, value, 0.0), axis=0, keepdims=True
            )
        reply_send[g, 3:8, :] = jnp.zeros((5, records), f32)

    @pl.loop(1, groups)
    def _(step):
        answer(lax.rem(me + step, groups))
        reply_copy(step).start()

    answer(me)
    reply_got[me] = reply_send[me]
    for sweep in range(SWEEPS):
        add_wall(sweep, ni - 1, ni - 2)
        sweep_c(sweep, SWEEPS - sweep if sweep < SWEEPS - 1 else 1, ni - 1)

    for step in range(1, groups):
        reply_copy(step).wait_recv()
    total = lax.fori_loop(
        0, groups, lambda g, kept: kept + reply_got[g], jnp.zeros((SUB, records), f32)
    )
    weighted = jnp.concatenate(split3(total[0:3] * weights), axis=0)
    out = lax.dot_general(
        weighted, onehot_s, (((1,), (1,)), ((), ())), preferred_element_type=f32
    )
    sens_o[...] = out[0:3] + out[3:6] + out[6:9]
    for step in range(1, groups):
        reply_copy(step).wait_send()
        rec_copy(step).wait_send()


def body(
    struct_disp,
    rec_struct,
    rec_block,
    rec_node,
    rec_weight,
    offset,
    prior_warp,
    inv_volume,
    coord_cot,
    vol_cot,
):
    groups = lax.axis_size("blocks")
    slabs = lax.axis_size("span")
    _, ni, nj, nk = offset.shape
    records = rec_struct.shape[0]
    f32 = jnp.float32
    rows_k = nj + 2 * SUB
    tiles = nk // LANES
    half = ni // 2

    def halo_rows4(comps):
        return [pltpu.VMEM((2, comps, half, SUB, nk), f32)] * 2

    def halo_lanes(comps, width):
        count = -(-comps * ni * width // LANES)
        return [
            pltpu.VMEM((2, count, nj, LANES), f32),
            pltpu.VMEM((2, count, rows_k, LANES), f32),
        ]

    vmem = pl.BlockSpec(memory_space=pltpu.VMEM)
    anywhere = pl.BlockSpec(memory_space=pl.ANY)
    outs = pl.pallas_call(
        functools.partial(kernel, groups, slabs),
        out_shape=(
            jax.ShapeDtypeStruct(offset.shape, f32),
            jax.ShapeDtypeStruct(offset.shape, f32),
            jax.ShapeDtypeStruct(struct_disp.shape, f32),
        ),
        in_specs=[vmem] * 5 + [anywhere] * 5,
        out_specs=[anywhere, vmem, vmem],
        scratch_shapes=[
            pltpu.VMEM((4, ni, tiles + 1, rows_k, LANES), f32),
            pltpu.VMEM((3, ni, tiles + 1, rows_k, LANES), f32),
            pltpu.VMEM((4, ni, tiles + 1, rows_k, LANES), f32),
            pltpu.VMEM((3, tiles, nj, LANES), f32),
            pltpu.VMEM((3, tiles, nj + SUB, LANES), f32),
            pltpu.VMEM((SUB, records), f32),
            pltpu.VMEM((groups, SUB, records), f32),
            pltpu.VMEM((groups, SUB, records), f32),
            pltpu.VMEM((groups, SUB, records), f32),
            *halo_rows4(4),
            *halo_lanes(4, SWEEPS),
            pltpu.VMEM((2, 3, rows_k, LANES), f32),
            *([pltpu.VMEM((2, 4, tiles, ni, LANES), f32)] * 2),
            *halo_lanes(4, 1),
            *halo_rows4(3),
            *halo_lanes(3, SWEEPS),
            pltpu.SemaphoreType.DMA((2, groups)),
            pltpu.SemaphoreType.DMA((2, groups)),
            pltpu.SemaphoreType.DMA((2, 7, 4)),
            pltpu.VMEM((3, ni, nj, nk), f32),
            pltpu.SemaphoreType.DMA((5, tiles)),
            pltpu.SemaphoreType.DMA((tiles,)),
        ],
        compiler_params=pltpu.CompilerParams(
            collective_id=0, has_side_effects=True, vmem_limit_bytes=VMEM_LIMIT
        ),
        name="warp_adjoint",
    )(
        rec_struct,
        rec_block.reshape(records),
        rec_node,
        rec_weight,
        struct_disp,
        offset,
        prior_warp,
        inv_volume,
        coord_cot,
        vol_cot,
    )
    return outs


def solution(mesh):
    placed = (
        P(None, ("blocks", "span")),
        P(("blocks", "span")),
        P(("blocks", "span"), None),
        P(("blocks", "span")),
        P(("blocks", "span")),
        P(None, None, "blocks", "span"),
        P(None, None, "blocks", "span"),
        P(None, "blocks", "span"),
        P(None, None, "blocks", "span"),
        P(None, "blocks", "span"),
    )
    return jax.shard_map(
        body,
        mesh=mesh,
        in_specs=placed,
        out_specs=(
            P(None, None, "blocks", "span"),
            P(None, None, "blocks", "span"),
            P(None, ("blocks", "span")),
        ),
        check_vma=False,
    )
```

profile of v0, /device:TPU:3, one launch (start us, length us, event | category | flops | bytes accessed | tf_op | source)
XLA Modules:
  0.0 70.4 jit_solution(2237702844296065150)
XLA Ops:
  0.6 65.1 %warp_adjoint.1 = (f32[3,16,32,256]{3,2,1,0:T(8,128)}, f32[3,16,32,256]{3,2,1,0:T(8,128)}, f32[3,512]{1,0:T(4,128)}) custom-call(s32[512]{0:T(512)} %struct_of.1, s32[512]{0:T(512)} %bitcast.1, s32[512]{0:T(512)} %node_of.1, f32[512]{0:T(512)} %weight_of.1, f32[3,512]{1,0:T(4,128)} %disp.1, f32[3,16,32,256]{3,2,1,0:T(8,128)} %offset_h.1, ...), custom_call_target="tpu_custom_call" | custom-call | tf_op jit(solution)/shard_map/warp_adjoint/pallas_call | solution.py:672
  65.8 0.0 copy-start
  65.8 2.8 %copy.16 = f32[3,16,32,256]{3,2,1,0:T(8,128)} copy(f32[3,16,32,256]{3,2,1,0:T(8,128)} %get-tuple-element.6) | data formatting | bytes 3145728
  68.6 0.0 copy-done
  68.6 0.0 copy-start.1
  68.6 1.1 %copy.17 = f32[3,16,32,256]{3,2,1,0:T(8,128)} copy(f32[3,16,32,256]{3,2,1,0:T(8,128)S(1)} %copy-done) | data formatting | bytes 3145728
  69.8 0.0 copy-done.1
  69.8 0.6 copy.18
Async XLA Ops:
  65.8 2.9 %copy-start = (f32[3,16,32,256]{3,2,1,0:T(8,128)S(1)}, f32[3,16,32,256]{3,2,1,0:T(8,128)}, u32[]{:S(2)}) copy-start(f32[3,16,32,256]{3,2,1,0:T(8,128)} %get-tuple-element.7) | copy-start | bytes 4718596
  68.6 1.1 %copy-start.1 = (f32[3,512]{1,0:T(4,128)S(1)}, f32[3,512]{1,0:T(4,128)}, u32[]{:S(2)}) copy-start(f32[3,512]{1,0:T(4,128)} %get-tuple-element.8) | copy-start | bytes 18436
where the time goes:
time: 70.6 us; the launch traced here: 70.4 us
  Pallas kernels  65.1 us (92%)
  local copies, waits for them, and re-layouts  4.59 us (7%)
    pallas_call x1, Pallas kernels, body(): pl.pallas_call(functools.partial(kernel, groups, slabs), out_shape=(jax.S...  65.1 us
    unnamed x7, local copies, waits for them, and re-layouts  4.59 us

commit v1 on v0

v1 whole, which is shorter than its diff:
```python
import functools

import jax
import jax.numpy as jnp
from jax import lax
from jax.experimental import pallas as pl
from jax.experimental.pallas import tpu as pltpu
from jax.sharding import PartitionSpec as P

SWEEPS = 4
WIDE = SWEEPS + 1
LANES = 128
SUB = 8
VMEM_LIMIT = 40 * 1024 * 1024
MESH = pl.DeviceIdType.MESH


def split3(x):
    hi = x.astype(jnp.bfloat16)
    rest = x - hi.astype(jnp.float32)
    mid = rest.astype(jnp.bfloat16)
    low = (rest - mid.astype(jnp.float32)).astype(jnp.bfloat16)
    return hi, mid, low


def iota(shape, dim):
    return lax.broadcasted_iota(jnp.int32, shape, dim)


def rows_plan(ni):
    inv = 3 * (ni - 1) * WIDE
    second = -(-(inv + (ni - 2) * SWEEPS) // SUB) * SUB
    total = second + -(-4 * ni // SUB) * SUB
    return inv, second, total


def columns(chunks, width):
    return -(-chunks // (LANES // width))


def kernel(
    groups,
    slabs,
    struct_h,
    block_h,
    node_h,
    weight_h,
    disp_h,
    offset_h,
    prior_h,
    inv_h,
    cot_h,
    vol_h,
    warp,
    adj,
    sens_o,
    v0,
    v1,
    v2,
    v3,
    inv,
    sb,
    low_i,
    low_j,
    rec_send,
    rec_got,
    reply_send,
    reply_got,
    ja_send,
    ja_got,
    ka_send,
    ka_got,
    surf_got,
    jc_send,
    jc_got,
    kc_send,
    kc_got,
    struct_of,
    block_of,
    node_of,
    weight_of,
    disp,
    sem_small,
    sem_rec,
    sem_reply,
    sem_halo,
    sem_in,
):
    ni, nj, nk = offset_h.shape[1:]
    tiles = nk // LANES
    every = tiles + 1
    own = slice(SUB, SUB + nj)
    top, end = slice(0, SUB), slice(SUB + nj, SUB + nj + SUB)
    all_rows = nj + 2 * SUB
    lanes_of = lambda t: slice(t * LANES, (t + 1) * LANES)
    records = struct_of.shape[0]
    f32, bf16 = jnp.float32, jnp.bfloat16
    me = lax.axis_index("blocks")
    my = lax.axis_index("span")
    zero = lax.div(me, groups)
    near = (me > 0, me < groups - 1, my > 0, my < slabs - 1)
    has = near + tuple(near[a] & near[2 + b] for a in (0, 1) for b in (0, 1))
    step_of = ((-1, 0), (1, 0), (0, -1), (0, 1), (-1, -1), (-1, 1), (1, -1), (1, 1))
    where_to = tuple((me + a, my + b) for a, b in step_of)
    back = (1, 0, 3, 2, 7, 6, 5, 4)

    def at(r, count=SUB):
        if r % SUB == 0:
            return slice(r, r + count)
        return pl.ds(zero + r, count)

    def load(number, src, dst):
        copies = []
        for t in range(tiles):
            copies.append(
                pltpu.make_async_copy(src(lanes_of(t)), dst(t), sem_in.at[number, t])
            )
            copies[-1].start()
        return copies

    small = [
        pltpu.make_async_copy(src, dst, sem_small.at[n])
        for n, (src, dst) in enumerate(
            (
                (struct_h, struct_of),
                (disp_h, disp),
                (weight_h, weight_of),
                (block_h, block_of),
                (node_h, node_of),
            )
        )
    ]
    for copy in small:
        copy.start()
    load_prior = load(0, lambda x: prior_h.at[:, :, :, x], lambda t: v0.at[:, :, t, own, :])
    load_inv = load(1, lambda x: inv_h.at[:, :, x], lambda t: inv.at[:, t, own, :])
    load_offset = load(2, lambda x: offset_h.at[:, :, :, x], lambda t: sb.at[0:3, :, t, own, :])
    load_vol = load(3, lambda x: vol_h.at[:, :, x], lambda t: sb.at[3, :, t, own, :])
    load_cot = load(4, lambda x: cot_h.at[:, :, :, x], lambda t: adj.at[:, :, t, own, :])

    def arrived(copies):
        for copy in copies:
            copy.wait()

    barrier = pltpu.get_barrier_semaphore()
    greeted = groups - 1
    for d in range(2, 8):
        greeted = greeted + has[d].astype(jnp.int32)

        @pl.when(has[d])
        def _(d=d):
            pl.semaphore_signal(barrier, inc=1, device_id=where_to[d], device_id_type=MESH)

    for step in range(1, groups):
        pl.semaphore_signal(
            barrier, inc=1, device_id=(lax.rem(me + step, groups), my), device_id_type=MESH
        )

    def flat(ref):
        return ref[...].reshape(1, records)

    arrived(small)
    weights = flat(weight_of)
    onehot_s = (iota((disp.shape[1], records), 0) == flat(struct_of)).astype(bf16)
    parts = jnp.concatenate(split3(disp[...]), axis=0)
    gathered = jnp.dot(parts, onehot_s, preferred_element_type=f32)
    rec_send[0:3, :] = (gathered[0:3] + gathered[3:6] + gathered[6:9]) * weights
    rec_send[3:4, :] = (flat(block_of) * (nj * nk) + flat(node_of)).astype(f32)

    lane = iota((SUB, LANES), 1)
    first_lane, last_lane, left_half = lane == 0, lane == LANES - 1, lane < LANES // 2
    tile_rows = [SUB + r * SUB for r in range(nj // SUB)]

    def pack_lanes(sources, send, column, width):
        per = LANES // width
        chunk = lane // width
        chunk_last = lax.rem(lane + width, LANES) // width
        for g in range(columns(len(sources), width)):
            first = [jnp.zeros((SUB, LANES), f32) for _ in tile_rows]
            last = list(first)
            for p, source in enumerate(sources[g * per : (g + 1) * per]):
                for n, r in enumerate(tile_rows):
                    both = jnp.where(left_half, source(0, r), source(tiles - 1, r))
                    if p:
                        both = pltpu.roll(both, p * width, 1)
                    first[n] = jnp.where(chunk == p, both, first[n])
                    last[n] = jnp.where(chunk_last == p, both, last[n])
            for n in range(len(tile_rows)):
                rows = slice(n * SUB, (n + 1) * SUB)
                send[0, column + g, rows, :] = first[n]
                send[1, column + g, rows, :] = last[n]

    def unpack_lanes(targets, got, column, width, rows):
        per = LANES // width
        chunk = lane // width
        for g in range(columns(len(targets), width)):
            after = [got[0, column + g, r : r + SUB, :] for r in rows]
            before = [got[1, column + g, r : r + SUB, :] for r in rows]
            for p, target in enumerate(targets[g * per : (g + 1) * per]):
                for n, r in enumerate(rows):
                    both = jnp.where(chunk == p, after[n], before[n])
                    if p:
                        both = pltpu.roll(both, LANES - p * width, 1)
                    target(r, both)

    def edge(ref, *index):
        return lambda t, r: ref[(*index, t, slice(r, r + SUB), slice(None))]

    def halo(ref, *index):
        def put(r, value):
            ref[(*index, tiles, slice(r, r + SUB), slice(None))] = value

        return put

    inv_at, second, total_rows = rows_plan(ni)
    field_layers = [(c, i) for c in range(3) for i in range(1, ni)]
    inner = range(1, ni - 1)
    shape_layers = [(c, i) for c in range(4) for i in range(ni)]
    near_columns = columns(len(field_layers) + len(inner), WIDE)

    def take_from(s, count):
        return SUB if s == 0 else SUB + nj - count

    def put_to(s, count):
        return SUB + nj if s == 0 else SUB - count

    def pack_rows(ref, index, send, start, count, first, stop, unroll):
        @pl.loop(first, stop, unroll=unroll)
        def _(i):
            for c, source in enumerate(ref):
                for s in (0, 1):
                    for t in range(tiles):
                        spot = pl.ds(start + (c * (stop - first) + i - first) * count, count)
                        send[s, t, spot, :] = source[(*index, i, t, at(take_from(s, count), count))]

    def unpack_rows(ref, got, start, count, first, stop, unroll):
        @pl.loop(first, stop, unroll=unroll)
        def _(i):
            for c, target in enumerate(ref):
                for s in (0, 1):
                    for t in range(tiles):
                        spot = pl.ds(start + (c * (stop - first) + i - first) * count, count)
                        target[i, t, at(put_to(s, count), count)] = got[s, t, spot, :]

    level = [v0, v1, v2, v3, warp]
    field = [level[0].at[c] for c in range(3)]
    shape = [sb.at[c] for c in range(4)]

    arrived(load_prior)
    arrived(load_inv)
    pack_rows(field, (), ja_send, 0, WIDE, 1, ni, 3)
    pack_rows([inv], (), ja_send, inv_at, SWEEPS, 1, ni - 1, 2)
    pack_lanes(
        [edge(v0, c, i) for c, i in field_layers] + [edge(inv, i) for i in inner],
        ka_send,
        0,
        WIDE,
    )
    arrived(load_offset)
    arrived(load_vol)
    pack_rows(shape, (), ja_send, second, 1, 0, ni, 2)
    pack_lanes([edge(sb, c, i) for c, i in shape_layers], ka_send, near_columns, 1)

    def move(d, src, dst, number):
        return pltpu.make_async_remote_copy(
            src_ref=src,
            dst_ref=dst,
            send_sem=sem_halo.at[0, number, d],
            recv_sem=sem_halo.at[1, number, d],
            device_id=where_to[d],
            device_id_type=MESH,
        )

    def start(d, *message):
        @pl.when(has[d])
        def _():
            move(d, *message).start()

    def received(d, *message):
        @pl.when(has[back[d]])
        def _():
            move(d, *message).wait_recv()

    def sent(d, *message):
        @pl.when(has[d])
        def _():
            move(d, *message).wait_send()

    def clear_missing(d, ref):
        @pl.when(jnp.logical_not(has[back[d]]))
        def _():
            ref[...] = jnp.zeros(ref.shape, f32)

    def row_message(d, send, got, rows, number):
        return (d, send.at[d, :, rows, :], got.at[d, :, rows, :], number)

    def lane_messages(send, got, number):
        out = []
        for s in (0, 1):
            out.append((2 + s, send.at[s], got.at[s, :, own, :], number))
        for a, rows, to in ((0, slice(0, SUB), end), (1, slice(nj - SUB, nj), top)):
            for s in (0, 1):
                out.append(
                    (4 + 2 * a + s, send.at[s, :, rows, :], got.at[s, :, to, :], number)
                )
        return out

    wide_rows = [row_message(d, ja_send, ja_got, slice(0, second), 0) for d in (0, 1)]
    thin_rows = [row_message(d, ja_send, ja_got, slice(second, total_rows), 1) for d in (0, 1)]
    lanes_a = lane_messages(ka_send, ka_got, 0)
    surf = [(2 + s, v0.at[:, 0, s * (tiles - 1)], surf_got.at[s], 2) for s in (0, 1)]
    rows_c = [row_message(d, jc_send, jc_got, slice(None), 3) for d in (0, 1)]
    lanes_c = lane_messages(kc_send, kc_got, 3)
    for d, _, dst, _ in wide_rows + thin_rows + lanes_a + surf + rows_c + lanes_c:
        clear_missing(d, dst)

    def rec_copy(step):
        return pltpu.make_async_remote_copy(
            src_ref=rec_send,
            dst_ref=rec_got.at[me],
            send_sem=sem_rec.at[0, step],
            recv_sem=sem_rec.at[1, step],
            device_id=(lax.rem(me + step, groups), my),
            device_id_type=MESH,
        )

    pl.semaphore_wait(barrier, greeted)
    for message in lanes_a + wide_rows:
        start(*message)
    for step in range(1, groups):
        rec_copy(step).start()
    for message in thin_rows:
        start(*message)
    rec_got[me] = rec_send[...]

    def in_pairs(first, stop):
        def run(step):
            even = first + (stop - first) // 2 * 2
            if even > first:
                pl.loop(first, even, unroll=2)(step)
            if even < stop:
                step(even)

        return run

    def changes(src, c, i, r, count):
        x = [src[c, i, t, at(r), :] for t in range(every)]
        right = [pltpu.roll(a, 1, 1) for a in x]
        left = [pltpu.roll(a, LANES - 1, 1) for a in x]
        out = []
        for t in range(count):
            total = jnp.where(first_lane, right[t - 1], right[t])
            total = total + jnp.where(last_lane, left[(t + 1) % every], left[t])
            total = total + (src[c, i, t, at(r - 1), :] + src[c, i, t, at(r + 1), :])
            total = total + (src[c, i - 1, t, at(r), :] + src[c, i + 1, t, at(r), :])
            out.append(total - 6.0 * x[t])
        return x, out

    def sweep_a(s, first, stop, rows):
        src, dst = level[s], level[s + 1]

        @in_pairs(first, stop)
        def _(i):
            for c in range(3):
                for r in rows:
                    x, change = changes(src, c, i, r, every)
                    for t in range(every):
                        dst[c, i, t, at(r), :] = x[t] + inv[i, t, at(r), :] * change[t]

    def keep_layer(i, rows):
        for c in range(3):
            value = level[0][c, i, :, rows, :]
            for s in range(1, SWEEPS + 1):
                level[s][c, i, :, rows, :] = value

    low_row, high_row = SUB - SWEEPS, SUB + nj - SWEEPS
    outer_rows = (low_row, high_row)
    shifted_rows = list(range(low_row, high_row + 1, SUB))
    field_halos = [halo(v0, c, i) for c, i in field_layers] + [halo(inv, i) for i in inner]
    shape_halos = [halo(sb, c, i) for c, i in shape_layers]

    for message in lanes_a[:2]:
        received(*message)
    unpack_lanes(field_halos, ka_got, 0, WIDE, tile_rows)
    keep_layer(ni - 1, own)
    for s in range(SWEEPS):
        sweep_a(s, s + 2, ni - 1, tile_rows)

    row_of = (me * nj + iota((all_rows, records), 0) - SUB).astype(f32)
    col_of = iota((nk, records), 0).astype(f32)

    def target_of(code):
        row = jnp.floor((code + 0.5) * (1.0 / nk))
        return row, code - row * nk

    def scatter(g, total):
        got = rec_got[g]
        row, col = target_of(got[3:4, :])
        here = row_of == row
        cols = (col_of == col).astype(bf16)
        pieces = split3(got[0:3, :])
        left = jnp.concatenate(
            [
                jnp.where(here, pieces[n][c : c + 1, :].astype(f32), 0.0)
                for n in range(3)
                for c in range(3)
            ],
            axis=0,
        ).astype(bf16)
        out = lax.dot_general(
            left, cols, (((1,), (1,)), ((), ())), preferred_element_type=f32
        )
        rows = 3 * all_rows
        return total + (out[0:rows] + out[rows : 2 * rows] + out[2 * rows :])

    def scatter_next(step, total):
        rec_copy(step).wait_recv()
        return scatter(lax.rem(me - step + groups, groups), total)

    surface = scatter(me, jnp.zeros((3 * all_rows, nk), f32))
    surface = lax.fori_loop(1, groups, scatter_next, surface)
    for c in range(3):
        for t in range(tiles):
            v0[c, 0, t] = surface[c * all_rows : (c + 1) * all_rows, lanes_of(t)]
    for message in surf:
        start(*message)

    for message in wide_rows + lanes_a[2:]:
        received(*message)
    unpack_rows(field, ja_got, 0, WIDE, 1, ni, 3)
    unpack_rows([inv], ja_got, inv_at, SWEEPS, 1, ni - 1, 2)
    unpack_lanes(field_halos, ka_got, 0, WIDE, (0, SUB + nj))
    for rows in (top, end):
        keep_layer(ni - 1, rows)
    for s in range(SWEEPS):
        sweep_a(s, s + 2, ni - 1, outer_rows)

    for message in surf:
        received(*message)
    for c in range(3):
        for r in range(0, all_rows, SUB):
            rows = slice(r, r + SUB)
            v0[c, 0, tiles, rows, :] = jnp.where(
                left_half, surf_got[0, c, rows, :], surf_got[1, c, rows, :]
            )
    keep_layer(0, slice(0, all_rows))
    for s in range(SWEEPS):
        sweep_a(s, 1, s + 2, shifted_rows)

    for message in thin_rows:
        received(*message)
    unpack_rows(shape, ja_got, second, 1, 0, ni, 2)
    unpack_lanes(shape_halos, ka_got, near_columns, 1, range(0, all_rows, SUB))

    for r in shifted_rows:
        row_at = me * nj + iota((SUB, LANES), 0) + (r - SUB)
        row_in = (row_at >= 0) & (row_at < groups * nj - 1)
        for t in range(every):
            col_at = my * nk + lane + (t * LANES if t < tiles else -LANES)
            cell = row_in & (col_at >= 0) & (col_at < slabs * nk - 1)

            @pl.loop(0, ni, unroll=4)
            def _(i, r=r, t=t, cell=cell):
                for c in range(3):
                    sb[c, i, t, at(r), :] = sb[c, i, t, at(r), :] + warp[c, i, t, at(r), :]
                keep = cell & (i < ni - 1)
                sb[3, i, t, at(r), :] = jnp.where(keep, sb[3, i, t, at(r), :], 0.0)

    def cross(a, b):
        return (
            a[1] * b[2] - a[2] * b[1],
            a[2] * b[0] - a[0] * b[2],
            a[0] * b[1] - a[1] * b[0],
        )

    low_i[...] = jnp.zeros(low_i.shape, f32)
    arrived(load_cot)
    for message in surf:
        sent(*message)

    @pl.loop(0, ni)
    def _(i):
        above = jnp.minimum(i + 1, ni - 1)
        for r in [0] + tile_rows:
            held = None
            order = range(tiles) if r == 0 else (tiles, *range(tiles))
            for t in order:
                base = [sb[c, i, t, at(r), :] for c in range(3)]
                edge_i = [sb[c, above, t, at(r), :] - base[c] for c in range(3)]
                edge_i[0] = edge_i[0] + 1.0
                weight = sb[3, i, t, at(r), :]
                weighted_i = [weight * e for e in edge_i]
                if r > 0:
                    edge_j = [sb[c, i, t, at(r + 1), :] - base[c] for c in range(3)]
                    edge_j[1] = edge_j[1] + 1.0
                    grad_k = cross(weighted_i, edge_j)
                    moved_k = [pltpu.roll(g, 1, 1) for g in grad_k]
                if t < tiles:
                    follow = (t + 1) % every
                    edge_k = [
                        jnp.where(
                            last_lane,
                            pltpu.roll(sb[c, i, follow, at(r), :], LANES - 1, 1),
                            pltpu.roll(base[c], LANES - 1, 1),
                        )
                        - base[c]
                        for c in range(3)
                    ]
                    edge_k[2] = edge_k[2] + 1.0
                    grad_j = cross(edge_k, weighted_i)
                    for c in range(3):
                        low_j[c, t, at(r), :] = grad_j[c]
                if r > 0 and t < tiles:
                    grad_i = cross([weight * e for e in edge_j], edge_k)
                    rate = jnp.where((i > 0) & (i < ni - 1), inv[i, t, at(r), :], 0.0)
                    for c in range(3):
                        lower_k = jnp.where(first_lane, held[c], moved_k[c])
                        out = adj[c, i, t, at(r), :] - grad_i[c] + low_i[c, t, at(r), :]
                        out = out + (low_j[c, t, at(r - 1), :] - grad_j[c])
                        out = out + (lower_k - grad_k[c])
                        low_i[c, t, at(r), :] = grad_i[c]
                        adj[c, i, t, at(r), :] = out
                        v0[c, i, t, at(r), :] = rate * out
                if r > 0:
                    held = moved_k

    flux_layers = [(c, i) for c in range(3) for i in inner]
    pack_rows(field, (), jc_send, 0, SWEEPS, 1, ni - 1, 2)
    for message in rows_c:
        start(*message)
    pack_lanes([edge(v0, c, i) for c, i in flux_layers], kc_send, 0, SWEEPS)
    for message in lanes_c:
        start(*message)
    for s in range(SWEEPS):
        for c in range(3):
            for i in (0, ni - 1):
                level[s][c, i] = jnp.zeros(v0.shape[2:], f32)

    def sweep_c(s, first, stop, rows, adds):
        src = level[s]
        last = s == SWEEPS - 1

        @in_pairs(first, stop)
        def _(i):
            for c in range(3):
                for r, (low, high) in zip(rows, adds):
                    x, change = changes(src, c, i, r, tiles if last else every)
                    for t, delta in enumerate(change):
                        if t < tiles:
                            to = at(r + low, high - low)
                            adj[c, i, t, to, :] = adj[c, i, t, to, :] + delta[low:high]
                        if not last:
                            level[s + 1][c, i, t, at(r), :] = (
                                x[t] + inv[i, t, at(r), :] * delta
                            )

    whole = (0, SUB)
    flux_halos = [halo(v0, c, i) for c, i in flux_layers]
    for message in lanes_c[:2]:
        received(*message)
    unpack_lanes(flux_halos, kc_got, 0, SWEEPS, tile_rows)
    inner_adds = [whole] * len(tile_rows)
    inner_adds[0] = (SWEEPS, SUB)
    inner_adds[-1] = (0, SUB - SWEEPS)
    for s in range(SWEEPS - 1):
        sweep_c(s, 1, ni - 1, tile_rows, inner_adds)
    mid_rows = shifted_rows[1:-1]
    sweep_c(SWEEPS - 1, 1, ni - 1, mid_rows, [whole] * len(mid_rows))

    for message in rows_c + lanes_c[2:]:
        received(*message)
    unpack_rows(field, jc_got, 0, SWEEPS, 1, ni - 1, 2)
    unpack_lanes(flux_halos, kc_got, 0, SWEEPS, (0, SUB + nj))
    for s in range(SWEEPS - 1):
        sweep_c(s, 1, SWEEPS - s, outer_rows, [whole] * 2)

    def add_wall(wall, layer):
        for c in range(3):
            for t in range(tiles):
                for r in tile_rows:
                    value = adj[c, wall, t, at(r), :]
                    for s in range(SWEEPS):
                        value = value + level[s][c, layer, t, at(r), :]
                    adj[c, wall, t, at(r), :] = value

    add_wall(0, 1)

    def wall_of(c):
        return jnp.concatenate([adj[c, 0, t, own, :] for t in range(tiles)], axis=1)

    wall = jnp.concatenate(
        [jnp.concatenate(split3(wall_of(c)), axis=0) for c in range(3)], axis=0
    )
    row_w = (me * nj + iota((nj, records), 0)).astype(f32)

    def reply_copy(step):
        to = lax.rem(me + step, groups)
        return pltpu.make_async_remote_copy(
            src_ref=reply_send.at[to],
            dst_ref=reply_got.at[me],
            send_sem=sem_reply.at[0, step],
            recv_sem=sem_reply.at[1, step],
            device_id=(to, my),
            device_id_type=MESH,
        )

    def answer(g):
        row, col = target_of(rec_got[g, 3:4, :])
        cols = (col_of == col).astype(bf16)
        here = row_w == row
        out = jnp.dot(wall, cols, preferred_element_type=f32)
        for c in range(3):
            first = 3 * c * nj
            value = (
                out[first : first + nj]
                + out[first + nj : first + 2 * nj]
                + out[first + 2 * nj : first + 3 * nj]
            )
            reply_send[g, c : c + 1, :] = jnp.sum(
                jnp.where(here, value, 0.0), axis=0, keepdims=True
            )
        reply_send[g, 3:4, :] = jnp.zeros((1, records), f32)

    @pl.loop(1, groups)
    def _(step):
        answer(lax.rem(me + step, groups))
        reply_copy(step).start()

    answer(me)
    reply_got[me] = reply_send[me]

    for s in range(SWEEPS - 1):
        sweep_c(s, SWEEPS - s, ni - 1, outer_rows, [whole] * 2)
    sweep_c(SWEEPS - 1, 1, ni - 1, outer_rows, [whole] * 2)
    add_wall(ni - 1, ni - 2)

    for step in range(1, groups):
        reply_copy(step).wait_recv()
    total = lax.fori_loop(
        0, groups, lambda g, kept: kept + reply_got[g], jnp.zeros((4, records), f32)
    )
    weighted = jnp.concatenate(split3(total[0:3] * weights), axis=0)
    out = lax.dot_general(
        weighted, onehot_s, (((1,), (1,)), ((), ())), preferred_element_type=f32
    )
    sens_o[...] = out[0:3] + out[3:6] + out[6:9]
    for message in wide_rows + thin_rows + lanes_a + rows_c + lanes_c:
        sent(*message)
    for step in range(1, groups):
        reply_copy(step).wait_send()
        rec_copy(step).wait_send()


def deliver(warp, adj, sens, warp_h, adj_h, sens_h, sem):
    nj, nk = warp_h.shape[2:]
    own = slice(SUB, SUB + nj)
    copies = []
    for t in range(nk // LANES):
        lanes = slice(t * LANES, (t + 1) * LANES)
        for n, (src, dst) in enumerate(((warp, warp_h), (adj, adj_h))):
            copies.append(
                pltpu.make_async_copy(
                    src.at[:, :, t, own, :], dst.at[:, :, :, lanes], sem.at[n, t]
                )
            )
    for copy in copies:
        copy.start()
    sens_h[...] = sens[...]
    for copy in copies:
        copy.wait()


def body(
    struct_disp,
    rec_struct,
    rec_block,
    rec_node,
    rec_weight,
    offset,
    prior_warp,
    inv_volume,
    coord_cot,
    vol_cot,
):
    groups = lax.axis_size("blocks")
    slabs = lax.axis_size("span")
    _, ni, nj, nk = offset.shape
    records = rec_struct.shape[0]
    f32 = jnp.float32
    all_rows = nj + 2 * SUB
    tiles = nk // LANES
    _, _, total_rows = rows_plan(ni)
    cols_a = columns(3 * (ni - 1) + ni - 2, WIDE) + columns(4 * ni, 1)
    cols_c = columns(3 * (ni - 2), SWEEPS)
    rows_c = -(-3 * (ni - 2) * SWEEPS // SUB) * SUB

    def lane_buffers(count):
        return [
            pltpu.VMEM((2, count, nj, LANES), f32),
            pltpu.VMEM((2, count, all_rows, LANES), f32),
        ]

    vmem = pl.BlockSpec(memory_space=pltpu.VMEM)
    hbm = pl.BlockSpec(memory_space=pltpu.HBM)
    in_place = lambda x: pltpu.with_memory_space_constraint(x, pltpu.HBM)
    warp, adj, sens = pl.pallas_call(
        functools.partial(kernel, groups, slabs),
        out_shape=(
            pltpu.VMEM((3, ni, tiles + 1, all_rows, LANES), f32),
            pltpu.VMEM((3, ni, tiles, all_rows, LANES), f32),
            pltpu.VMEM(struct_disp.shape, f32),
        ),
        in_specs=[hbm] * 10,
        out_specs=[vmem] * 3,
        scratch_shapes=[
            *([pltpu.VMEM((3, ni, tiles + 1, all_rows, LANES), f32)] * SWEEPS),
            pltpu.VMEM((ni, tiles + 1, all_rows, LANES), f32),
            pltpu.VMEM((4, ni, tiles + 1, all_rows, LANES), f32),
            pltpu.VMEM((3, tiles, nj + SUB, LANES), f32),
            pltpu.VMEM((3, tiles, nj + SUB, LANES), f32),
            pltpu.VMEM((4, records), f32),
            pltpu.VMEM((groups, 4, records), f32),
            pltpu.VMEM((groups, 4, records), f32),
            pltpu.VMEM((groups, 4, records), f32),
            *([pltpu.VMEM((2, tiles, total_rows, LANES), f32)] * 2),
            *lane_buffers(cols_a),
            pltpu.VMEM((2, 3, all_rows, LANES), f32),
            *([pltpu.VMEM((2, tiles, rows_c, LANES), f32)] * 2),
            *lane_buffers(cols_c),
            *([pltpu.VMEM((records,), jnp.int32)] * 3),
            pltpu.VMEM((records,), f32),
            pltpu.VMEM(struct_disp.shape, f32),
            pltpu.SemaphoreType.DMA((5,)),
            pltpu.SemaphoreType.DMA((2, groups)),
            pltpu.SemaphoreType.DMA((2, groups)),
            pltpu.SemaphoreType.DMA((2, 4, 8)),
            pltpu.SemaphoreType.DMA((5, tiles)),
        ],
        compiler_params=pltpu.CompilerParams(
            collective_id=0, has_side_effects=True, vmem_limit_bytes=VMEM_LIMIT
        ),
        name="warp_adjoint",
    )(
        *map(
            in_place,
            (
                rec_struct,
                rec_block.reshape(records),
                rec_node,
                rec_weight,
                struct_disp,
                offset,
                prior_warp,
                inv_volume,
                coord_cot,
                vol_cot,
            ),
        )
    )
    return pl.pallas_call(
        deliver,
        out_shape=(
            jax.ShapeDtypeStruct(offset.shape, f32),
            jax.ShapeDtypeStruct(offset.shape, f32),
            jax.ShapeDtypeStruct(struct_disp.shape, f32),
        ),
        in_specs=[vmem] * 3,
        out_specs=[hbm, hbm, vmem],
        scratch_shapes=[pltpu.SemaphoreType.DMA((2, tiles))],
        compiler_params=pltpu.CompilerParams(vmem_limit_bytes=4 * 1024 * 1024),
        name="deliver",
    )(warp, adj, sens)


def solution(mesh):
    placed = (
        P(None, ("blocks", "span")),
        P(("blocks", "span")),
        P(("blocks", "span"), None),
        P(("blocks", "span")),
        P(("blocks", "span")),
        P(None, None, "blocks", "span"),
        P(None, None, "blocks", "span"),
        P(None, "blocks", "span"),
        P(None, None, "blocks", "span"),
        P(None, "blocks", "span"),
    )
    return jax.shard_map(
        body,
        mesh=mesh,
        in_specs=placed,
        out_specs=(
            P(None, None, "blocks", "span"),
            P(None, None, "blocks", "span"),
            P(None, ("blocks", "span")),
        ),
        check_vma=False,
    )
```

time: 70.6 us -> 55.1 us (0.78)
  the two profiles are of different devices: /device:TPU:3 before, /device:TPU:0 now
where the time goes in v1:
time: 55.1 us; the launch traced here: 54.3 us
  Pallas kernels  53.7 us (97%)
  between operations  0.64 us (1%)
    pallas_call x1, Pallas kernels, body(): pl.pallas_call(functools.partial(kernel, groups, slabs), out_shape=(pltpu...  51.4 us
    pallas_call x1, Pallas kernels, body(): pl.pallas_call(deliver, out_shape=(jax.ShapeDtypeStruct(offset.shape, f32...  2.29 us

profile of v1, /device:TPU:0, one launch (start us, length us, event | category | flops | bytes accessed | tf_op | source)
XLA Modules:
  0.0 54.3 jit_solution(174863117040797752)
XLA Ops:
  0.6 51.4 %warp_adjoint.1 = (f32[3,16,3,48,128]{4,3,2,1,0:T(8,128)S(1)}, f32[3,16,2,48,128]{4,3,2,1,0:T(8,128)S(1)}, f32[3,512]{1,0:T(4,128)S(1)}) custom-call(s32[512]{0:T(512)} %struct_h.1, s32[512]{0:T(512)} %bitcast.1, s32[512]{0:T(512)} %node_h.1, f32[512]{0:T(512)} %weight_h.1, f32[3,512]{1,0:T(4,128)} %disp_h.1, f32[3,16,32,256]{3,2,1,0:T(8,128)} %offset_h.1, ...), custom_call_target="tpu_custom_call" | custom-call | tf_op jit(solution)/shard_map/warp_adjoint/pallas_call | solution.py:706
  52.0 2.3 %deliver.1 = (f32[3,16,32,256]{3,2,1,0:T(8,128)}, f32[3,16,32,256]{3,2,1,0:T(8,128)}, f32[3,512]{1,0:T(4,128)}) custom-call(f32[3,16,3,48,128]{4,3,2,1,0:T(8,128)S(1)} %get-tuple-element.6.warp, f32[3,16,2,48,128]{4,3,2,1,0:T(8,128)S(1)} %get-tuple-element.7.adj, f32[3,512]{1,0:T(4,128)S(1)} %get-tuple-element.8.sens), custom_call_target="tpu_custom_call" | custom-call | tf_op jit(solution)/shard_map/deliver/pallas_call | solution.py:760

commit v2 on v1

--- a/solution.py
+++ b/solution.py
@@ -109,6 +109,24 @@
             return slice(r, r + count)
         return pl.ds(zero + r, count)
 
+    def arrived(copies):
+        for copy in copies:
+            copy.wait()
+
+    barrier = pltpu.get_barrier_semaphore()
+    greeted = groups - 1
+    for d in range(2, 8):
+        greeted = greeted + has[d].astype(jnp.int32)
+
+        @pl.when(has[d])
+        def _(d=d):
+            pl.semaphore_signal(barrier, inc=1, device_id=where_to[d], device_id_type=MESH)
+
+    for step in range(1, groups):
+        pl.semaphore_signal(
+            barrier, inc=1, device_id=(lax.rem(me + step, groups), my), device_id_type=MESH
+        )
+
     def load(number, src, dst):
         copies = []
         for t in range(tiles):
@@ -138,24 +156,6 @@
     load_vol = load(3, lambda x: vol_h.at[:, :, x], lambda t: sb.at[3, :, t, own, :])
     load_cot = load(4, lambda x: cot_h.at[:, :, :, x], lambda t: adj.at[:, :, t, own, :])
 
-    def arrived(copies):
-        for copy in copies:
-            copy.wait()
-
-    barrier = pltpu.get_barrier_semaphore()
-    greeted = groups - 1
-    for d in range(2, 8):
-        greeted = greeted + has[d].astype(jnp.int32)
-
-        @pl.when(has[d])
-        def _(d=d):
-            pl.semaphore_signal(barrier, inc=1, device_id=where_to[d], device_id_type=MESH)
-
-    for step in range(1, groups):
-        pl.semaphore_signal(
-            barrier, inc=1, device_id=(lax.rem(me + step, groups), my), device_id_type=MESH
-        )
-
     def flat(ref):
         return ref[...].reshape(1, records)
 
@@ -224,20 +224,20 @@
     def put_to(s, count):
         return SUB + nj if s == 0 else SUB - count
 
-    def pack_rows(ref, index, send, start, count, first, stop, unroll):
+    def pack_rows(ref, send, start, count, first, stop, unroll, sides=(0, 1)):
         @pl.loop(first, stop, unroll=unroll)
         def _(i):
             for c, source in enumerate(ref):
-                for s in (0, 1):
+                for s in sides:
                     for t in range(tiles):
                         spot = pl.ds(start + (c * (stop - first) + i - first) * count, count)
-                        send[s, t, spot, :] = source[(*index, i, t, at(take_from(s, count), count))]
-
-    def unpack_rows(ref, got, start, count, first, stop, unroll):
+                        send[s, t, spot, :] = source[i, t, at(take_from(s, count), count)]
+
+    def unpack_rows(ref, got, start, count, first, stop, unroll, sides=(0, 1)):
         @pl.loop(first, stop, unroll=unroll)
         def _(i):
             for c, target in enumerate(ref):
-                for s in (0, 1):
+                for s in sides:
                     for t in range(tiles):
                         spot = pl.ds(start + (c * (stop - first) + i - first) * count, count)
                         target[i, t, at(put_to(s, count), count)] = got[s, t, spot, :]
@@ -245,21 +245,6 @@
     level = [v0, v1, v2, v3, warp]
     field = [level[0].at[c] for c in range(3)]
     shape = [sb.at[c] for c in range(4)]
-
-    arrived(load_prior)
-    arrived(load_inv)
-    pack_rows(field, (), ja_send, 0, WIDE, 1, ni, 3)
-    pack_rows([inv], (), ja_send, inv_at, SWEEPS, 1, ni - 1, 2)
-    pack_lanes(
-        [edge(v0, c, i) for c, i in field_layers] + [edge(inv, i) for i in inner],
-        ka_send,
-        0,
-        WIDE,
-    )
-    arrived(load_offset)
-    arrived(load_vol)
-    pack_rows(shape, (), ja_send, second, 1, 0, ni, 2)
-    pack_lanes([edge(sb, c, i) for c, i in shape_layers], ka_send, near_columns, 1)
 
     def move(d, src, dst, number):
         return pltpu.make_async_remote_copy(
@@ -311,9 +296,6 @@
     surf = [(2 + s, v0.at[:, 0, s * (tiles - 1)], surf_got.at[s], 2) for s in (0, 1)]
     rows_c = [row_message(d, jc_send, jc_got, slice(None), 3) for d in (0, 1)]
     lanes_c = lane_messages(kc_send, kc_got, 3)
-    for d, _, dst, _ in wide_rows + thin_rows + lanes_a + surf + rows_c + lanes_c:
-        clear_missing(d, dst)
-
     def rec_copy(step):
         return pltpu.make_async_remote_copy(
             src_ref=rec_send,
@@ -324,20 +306,38 @@
             device_id_type=MESH,
         )
 
+    arrived(load_prior)
+    pack_rows(field, ja_send, 0, WIDE, 1, ni, 3)
+    arrived(load_inv)
+    pack_rows([inv], ja_send, inv_at, SWEEPS, 1, ni - 1, 2)
     pl.semaphore_wait(barrier, greeted)
-    for message in lanes_a + wide_rows:
-        start(*message)
     for step in range(1, groups):
         rec_copy(step).start()
-    for message in thin_rows:
+    start(*wide_rows[0])
+    pack_lanes(
+        [edge(v0, c, i) for c, i in field_layers] + [edge(inv, i) for i in inner],
+        ka_send,
+        0,
+        WIDE,
+    )
+    arrived(load_offset)
+    arrived(load_vol)
+    pack_lanes([edge(sb, c, i) for c, i in shape_layers], ka_send, near_columns, 1)
+    for message in lanes_a[:2]:
+        start(*message)
+    pack_rows(shape, ja_send, second, 1, 0, ni, 2)
+    for message in (thin_rows[0], *lanes_a[2:4], wide_rows[1], thin_rows[1], *lanes_a[4:]):
         start(*message)
     rec_got[me] = rec_send[...]
+    for d, _, dst, _ in wide_rows + thin_rows + lanes_a + surf + rows_c + lanes_c:
+        clear_missing(d, dst)
 
     def in_pairs(first, stop):
         def run(step):
-            even = first + (stop - first) // 2 * 2
-            if even > first:
-                pl.loop(first, even, unroll=2)(step)
+            unroll = (stop - first) // 2
+            even = first + 2 * unroll
+            if unroll:
+                pl.loop(first, even, unroll=unroll)(step)
             if even < stop:
                 step(even)
 
@@ -345,12 +345,22 @@
 
     def changes(src, c, i, r, count):
         x = [src[c, i, t, at(r), :] for t in range(every)]
-        right = [pltpu.roll(a, 1, 1) for a in x]
-        left = [pltpu.roll(a, LANES - 1, 1) for a in x]
+        if count == tiles:
+            nexts = [(x[t - 1], x[t], x[(t + 1) % every]) for t in range(tiles)]
+            before = [pltpu.roll(jnp.where(last_lane, a, b), 1, 1) for a, b, _ in nexts]
+            after = [
+                pltpu.roll(jnp.where(first_lane, d, b), LANES - 1, 1) for _, b, d in nexts
+            ]
+        else:
+            right = [pltpu.roll(a, 1, 1) for a in x]
+            left = [pltpu.roll(a, LANES - 1, 1) for a in x]
+            before = [jnp.where(first_lane, right[t - 1], right[t]) for t in range(every)]
+            after = [
+                jnp.where(last_lane, left[(t + 1) % every], left[t]) for t in range(every)
+            ]
         out = []
         for t in range(count):
-            total = jnp.where(first_lane, right[t - 1], right[t])
-            total = total + jnp.where(last_lane, left[(t + 1) % every], left[t])
+            total = before[t] + after[t]
             total = total + (src[c, i, t, at(r - 1), :] + src[c, i, t, at(r + 1), :])
             total = total + (src[c, i - 1, t, at(r), :] + src[c, i + 1, t, at(r), :])
             out.append(total - 6.0 * x[t])
@@ -386,15 +396,20 @@
     for s in range(SWEEPS):
         sweep_a(s, s + 2, ni - 1, tile_rows)
 
-    row_of = (me * nj + iota((all_rows, records), 0) - SUB).astype(f32)
-    col_of = iota((nk, records), 0).astype(f32)
-
     def target_of(code):
         row = jnp.floor((code + 0.5) * (1.0 / nk))
         return row, code - row * nk
 
-    def scatter(g, total):
-        got = rec_got[g]
+    together = 2 if groups % 2 == 0 and records <= 4 * LANES else 1
+
+    def side_by_side(parts):
+        return parts[0] if len(parts) == 1 else jnp.concatenate(parts, axis=1)
+
+    row_of = (me * nj + iota((all_rows, together * records), 0) - SUB).astype(f32)
+    col_of = iota((nk, together * records), 0).astype(f32)
+
+    def scatter(members, total):
+        got = side_by_side([rec_got[g] for g in members])
         row, col = target_of(got[3:4, :])
         here = row_of == row
         cols = (col_of == col).astype(bf16)
@@ -413,28 +428,56 @@
         rows = 3 * all_rows
         return total + (out[0:rows] + out[rows : 2 * rows] + out[2 * rows :])
 
-    def scatter_next(step, total):
+    def scatter_next(n, total):
+        steps = [n * together + k for k in range(together)]
+        for step in steps:
+            rec_copy(step).wait_recv()
+        return scatter([lax.rem(me - step + groups, groups) for step in steps], total)
+
+    for step in range(1, together):
         rec_copy(step).wait_recv()
-        return scatter(lax.rem(me - step + groups, groups), total)
-
-    surface = scatter(me, jnp.zeros((3 * all_rows, nk), f32))
-    surface = lax.fori_loop(1, groups, scatter_next, surface)
+    surface = scatter(
+        [lax.rem(me - step + groups, groups) for step in range(together)],
+        jnp.zeros((3 * all_rows, nk), f32),
+    )
+    surface = lax.fori_loop(1, groups // together, scatter_next, surface)
     for c in range(3):
         for t in range(tiles):
             v0[c, 0, t] = surface[c * all_rows : (c + 1) * all_rows, lanes_of(t)]
     for message in surf:
         start(*message)
 
-    for message in wide_rows + lanes_a[2:]:
-        received(*message)
-    unpack_rows(field, ja_got, 0, WIDE, 1, ni, 3)
-    unpack_rows([inv], ja_got, inv_at, SWEEPS, 1, ni - 1, 2)
-    unpack_lanes(field_halos, ka_got, 0, WIDE, (0, SUB + nj))
-    for rows in (top, end):
+    def outer(s):
+        rows = (end, top)[s]
+        for message in (wide_rows[s], thin_rows[s], *lanes_a[2 + 2 * s : 4 + 2 * s]):
+            received(*message)
+        unpack_rows(field, ja_got, 0, WIDE, 1, ni, 3, (s,))
+        unpack_rows([inv], ja_got, inv_at, SWEEPS, 1, ni - 1, 2, (s,))
+        unpack_lanes(field_halos, ka_got, 0, WIDE, (rows.start,))
+        unpack_rows(shape, ja_got, second, 1, 0, ni, 2, (s,))
+        unpack_lanes(shape_halos, ka_got, near_columns, 1, (rows.start,))
         keep_layer(ni - 1, rows)
+
+    def shape_rows(rows):
+        for r in rows:
+            row_at = me * nj + iota((SUB, LANES), 0) + (r - SUB)
+            row_in = (row_at >= 0) & (row_at < groups * nj - 1)
+            for t in range(every):
+                col_at = my * nk + lane + (t * LANES if t < tiles else -LANES)
+                cell = row_in & (col_at >= 0) & (col_at < slabs * nk - 1)
+
+                @pl.loop(0, ni, unroll=4)
+                def _(i, r=r, t=t, cell=cell):
+                    for c in range(3):
+                        sb[c, i, t, at(r), :] = sb[c, i, t, at(r), :] + warp[c, i, t, at(r), :]
+                    keep = cell & (i < ni - 1)
+                    sb[3, i, t, at(r), :] = jnp.where(keep, sb[3, i, t, at(r), :], 0.0)
+
+    outer(0)
     for s in range(SWEEPS):
-        sweep_a(s, s + 2, ni - 1, outer_rows)
-
+        sweep_a(s, s + 2, ni - 1, (high_row,))
+
+    unpack_lanes(shape_halos, ka_got, near_columns, 1, tile_rows)
     for message in surf:
         received(*message)
     for c in range(3):
@@ -445,26 +488,7 @@
             )
     keep_layer(0, slice(0, all_rows))
     for s in range(SWEEPS):
-        sweep_a(s, 1, s + 2, shifted_rows)
-
-    for message in thin_rows:
-        received(*message)
-    unpack_rows(shape, ja_got, second, 1, 0, ni, 2)
-    unpack_lanes(shape_halos, ka_got, near_columns, 1, range(0, all_rows, SUB))
-
-    for r in shifted_rows:
-        row_at = me * nj + iota((SUB, LANES), 0) + (r - SUB)
-        row_in = (row_at >= 0) & (row_at < groups * nj - 1)
-        for t in range(every):
-            col_at = my * nk + lane + (t * LANES if t < tiles else -LANES)
-            cell = row_in & (col_at >= 0) & (col_at < slabs * nk - 1)
-
-            @pl.loop(0, ni, unroll=4)
-            def _(i, r=r, t=t, cell=cell):
-                for c in range(3):
-                    sb[c, i, t, at(r), :] = sb[c, i, t, at(r), :] + warp[c, i, t, at(r), :]
-                keep = cell & (i < ni - 1)
-                sb[3, i, t, at(r), :] = jnp.where(keep, sb[3, i, t, at(r), :], 0.0)
+        sweep_a(s, 1, s + 2, tile_rows + [high_row])
 
     def cross(a, b):
         return (
@@ -475,59 +499,71 @@
 
     low_i[...] = jnp.zeros(low_i.shape, f32)
     arrived(load_cot)
+
+    def gradients(parts):
+        @pl.loop(0, ni, unroll=2)
+        def _(i):
+            above = jnp.minimum(i + 1, ni - 1)
+            for r, full in parts:
+                order = (tiles, *range(tiles)) if full else range(tiles)
+                base = [[sb[c, i, t, at(r), :] for c in range(3)] for t in range(every)]
+                held = None
+                for t in order:
+                    edge_i = [sb[c, above, t, at(r), :] - base[t][c] for c in range(3)]
+                    edge_i[0] = edge_i[0] + 1.0
+                    weight = sb[3, i, t, at(r), :]
+                    weighted_i = [weight * e for e in edge_i]
+                    if full:
+                        edge_j = [sb[c, i, t, at(r + 1), :] - base[t][c] for c in range(3)]
+                        edge_j[1] = edge_j[1] + 1.0
+                        grad_k = cross(weighted_i, edge_j)
+                    if t < tiles:
+                        follow = base[(t + 1) % every]
+                        edge_k = [
+                            pltpu.roll(
+                                jnp.where(first_lane, follow[c], base[t][c]), LANES - 1, 1
+                            )
+                            - base[t][c]
+                            for c in range(3)
+                        ]
+                        edge_k[2] = edge_k[2] + 1.0
+                        grad_j = cross(edge_k, weighted_i)
+                        for c in range(3):
+                            low_j[c, t, at(r), :] = grad_j[c]
+                    if full and t < tiles:
+                        grad_i = cross([weight * e for e in edge_j], edge_k)
+                        rate = jnp.where((i > 0) & (i < ni - 1), inv[i, t, at(r), :], 0.0)
+                        for c in range(3):
+                            lower_k = pltpu.roll(
+                                jnp.where(last_lane, held[c], grad_k[c]), 1, 1
+                            )
+                            out = adj[c, i, t, at(r), :] - grad_i[c] + low_i[c, t, at(r), :]
+                            out = out + (low_j[c, t, at(r - 1), :] - grad_j[c])
+                            out = out + (lower_k - grad_k[c])
+                            low_i[c, t, at(r), :] = grad_i[c]
+                            adj[c, i, t, at(r), :] = out
+                            v0[c, i, t, at(r), :] = rate * out
+                    if full:
+                        held = grad_k
+
+    flux_layers = [(c, i) for c in range(3) for i in inner]
+
+    def send_flux(s):
+        pack_rows(field, jc_send, 0, SWEEPS, 1, ni - 1, 2, (s,))
+        start(*rows_c[s])
+
     for message in surf:
         sent(*message)
-
-    @pl.loop(0, ni)
-    def _(i):
-        above = jnp.minimum(i + 1, ni - 1)
-        for r in [0] + tile_rows:
-            held = None
-            order = range(tiles) if r == 0 else (tiles, *range(tiles))
-            for t in order:
-                base = [sb[c, i, t, at(r), :] for c in range(3)]
-                edge_i = [sb[c, above, t, at(r), :] - base[c] for c in range(3)]
-                edge_i[0] = edge_i[0] + 1.0
-                weight = sb[3, i, t, at(r), :]
-                weighted_i = [weight * e for e in edge_i]
-                if r > 0:
-                    edge_j = [sb[c, i, t, at(r + 1), :] - base[c] for c in range(3)]
-                    edge_j[1] = edge_j[1] + 1.0
-                    grad_k = cross(weighted_i, edge_j)
-                    moved_k = [pltpu.roll(g, 1, 1) for g in grad_k]
-                if t < tiles:
-                    follow = (t + 1) % every
-                    edge_k = [
-                        jnp.where(
-                            last_lane,
-                            pltpu.roll(sb[c, i, follow, at(r), :], LANES - 1, 1),
-                            pltpu.roll(base[c], LANES - 1, 1),
-                        )
-                        - base[c]
-                        for c in range(3)
-                    ]
-                    edge_k[2] = edge_k[2] + 1.0
-                    grad_j = cross(edge_k, weighted_i)
-                    for c in range(3):
-                        low_j[c, t, at(r), :] = grad_j[c]
-                if r > 0 and t < tiles:
-                    grad_i = cross([weight * e for e in edge_j], edge_k)
-                    rate = jnp.where((i > 0) & (i < ni - 1), inv[i, t, at(r), :], 0.0)
-                    for c in range(3):
-                        lower_k = jnp.where(first_lane, held[c], moved_k[c])
-                        out = adj[c, i, t, at(r), :] - grad_i[c] + low_i[c, t, at(r), :]
-                        out = out + (low_j[c, t, at(r - 1), :] - grad_j[c])
-                        out = out + (lower_k - grad_k[c])
-                        low_i[c, t, at(r), :] = grad_i[c]
-                        adj[c, i, t, at(r), :] = out
-                        v0[c, i, t, at(r), :] = rate * out
-                if r > 0:
-                    held = moved_k
-
-    flux_layers = [(c, i) for c in range(3) for i in inner]
-    pack_rows(field, (), jc_send, 0, SWEEPS, 1, ni - 1, 2)
-    for message in rows_c:
-        start(*message)
+    shape_rows(shifted_rows[1:])
+    gradients([(tile_rows[0], False)] + [(r, True) for r in tile_rows[1:]])
+    send_flux(1)
+
+    outer(1)
+    for s in range(SWEEPS):
+        sweep_a(s, 1, ni - 1, (low_row,))
+    shape_rows(shifted_rows[:1])
+    gradients([(0, False), (tile_rows[0], True)])
+    send_flux(0)
     pack_lanes([edge(v0, c, i) for c, i in flux_layers], kc_send, 0, SWEEPS)
     for message in lanes_c:
         start(*message)
@@ -591,7 +627,7 @@
     wall = jnp.concatenate(
         [jnp.concatenate(split3(wall_of(c)), axis=0) for c in range(3)], axis=0
     )
-    row_w = (me * nj + iota((nj, records), 0)).astype(f32)
+    row_w = (me * nj + iota((nj, together * records), 0)).astype(f32)
 
     def reply_copy(step):
         to = lax.rem(me + step, groups)
@@ -604,8 +640,8 @@
             device_id_type=MESH,
         )
 
-    def answer(g):
-        row, col = target_of(rec_got[g, 3:4, :])
+    def answer(members):
+        row, col = target_of(side_by_side([rec_got[g, 3:4, :] for g in members]))
         cols = (col_of == col).astype(bf16)
         here = row_w == row
         out = jnp.dot(wall, cols, preferred_element_type=f32)
@@ -616,17 +652,23 @@
                 + out[first + nj : first + 2 * nj]
                 + out[first + 2 * nj : first + 3 * nj]
             )
-            reply_send[g, c : c + 1, :] = jnp.sum(
-                jnp.where(here, value, 0.0), axis=0, keepdims=True
-            )
-        reply_send[g, 3:4, :] = jnp.zeros((1, records), f32)
-
-    @pl.loop(1, groups)
-    def _(step):
-        answer(lax.rem(me + step, groups))
-        reply_copy(step).start()
-
-    answer(me)
+            found = jnp.sum(jnp.where(here, value, 0.0), axis=0, keepdims=True)
+            for n, g in enumerate(members):
+                reply_send[g, c : c + 1, :] = found[:, n * records : (n + 1) * records]
+        for g in members:
+            reply_send[g, 3:4, :] = jnp.zeros((1, records), f32)
+
+    def answer_next(n, last):
+        steps = [n * together + k + 1 for k in range(together)]
+        answer([lax.rem(me + step, groups) for step in steps])
+        for step in steps[: together - 1] if last else steps:
+            reply_copy(step).start()
+
+    @pl.loop(0, groups // together - 1)
+    def _(n):
+        answer_next(n, False)
+
+    answer_next(groups // together - 1, True)
     reply_got[me] = reply_send[me]
 
     for s in range(SWEEPS - 1):
@@ -655,16 +697,16 @@
     nj, nk = warp_h.shape[2:]
     own = slice(SUB, SUB + nj)
     copies = []
-    for t in range(nk // LANES):
-        lanes = slice(t * LANES, (t + 1) * LANES)
-        for n, (src, dst) in enumerate(((warp, warp_h), (adj, adj_h))):
-            copies.append(
-                pltpu.make_async_copy(
-                    src.at[:, :, t, own, :], dst.at[:, :, :, lanes], sem.at[n, t]
+    for n, (src, dst) in enumerate(((warp, warp_h), (adj, adj_h))):
+        for c in range(3):
+            for t in range(nk // LANES):
+                lanes = slice(t * LANES, (t + 1) * LANES)
+                copies.append(
+                    pltpu.make_async_copy(
+                        src.at[c, :, t, own, :], dst.at[c, :, :, lanes], sem.at[n, c, t]
+                    )
                 )
-            )
-    for copy in copies:
-        copy.start()
+                copies[-1].start()
     sens_h[...] = sens[...]
     for copy in copies:
         copy.wait()
@@ -766,7 +808,7 @@
         ),
         in_specs=[vmem] * 3,
         out_specs=[hbm, hbm, vmem],
-        scratch_shapes=[pltpu.SemaphoreType.DMA((2, tiles))],
+        scratch_shapes=[pltpu.SemaphoreType.DMA((2, 3, tiles))],
         compiler_params=pltpu.CompilerParams(vmem_limit_bytes=4 * 1024 * 1024),
         name="deliver",
     )(warp, adj, sens)

time: 55.1 us -> 50.8 us (0.922); the launches traced: 54.3 us -> 50.6 us
  Pallas kernels: 53.7 us -> 50 us
    pallas_call x1, Pallas kernels: 51.4 us -> 47.6 us  [body(): pl.pallas_call(functools.partial(kernel, groups, slabs), out_shape=(pltpu...]
where the time goes in v2:
time: 50.8 us; the launch traced here: 50.6 us
  Pallas kernels  50 us (98%)
  between operations  0.64 us (1%)
    pallas_call x1, Pallas kernels, body(): pl.pallas_call(functools.partial(kernel, groups, slabs), out_shape=(pltpu...  47.6 us
    pallas_call x1, Pallas kernels, body(): pl.pallas_call(deliver, out_shape=(jax.ShapeDtypeStruct(offset.shape, f32...  2.36 us

profile of v2, /device:TPU:0, one launch (start us, length us, event | category | flops | bytes accessed | tf_op | source)
XLA Modules:
  0.0 50.6 jit_solution(2103689102000598962)
XLA Ops:
  0.6 47.6 %warp_adjoint.1 = (f32[3,16,3,48,128]{4,3,2,1,0:T(8,128)S(1)}, f32[3,16,2,48,128]{4,3,2,1,0:T(8,128)S(1)}, f32[3,512]{1,0:T(4,128)S(1)}) custom-call(s32[512]{0:T(512)} %struct_h.1, s32[512]{0:T(512)} %bitcast.1, s32[512]{0:T(512)} %node_h.1, f32[512]{0:T(512)} %weight_h.1, f32[3,512]{1,0:T(4,128)} %disp_h.1, f32[3,16,32,256]{3,2,1,0:T(8,128)} %offset_h.1, ...), custom_call_target="tpu_custom_call" | custom-call | tf_op jit(solution)/shard_map/warp_adjoint/pallas_call | solution.py:748
  48.3 2.4 %deliver.1 = (f32[3,16,32,256]{3,2,1,0:T(8,128)}, f32[3,16,32,256]{3,2,1,0:T(8,128)}, f32[3,512]{1,0:T(4,128)}) custom-call(f32[3,16,3,48,128]{4,3,2,1,0:T(8,128)S(1)} %get-tuple-element.6.warp, f32[3,16,2,48,128]{4,3,2,1,0:T(8,128)S(1)} %get-tuple-element.7.adj, f32[3,512]{1,0:T(4,128)S(1)} %get-tuple-element.8.sens), custom_call_target="tpu_custom_call" | custom-call | tf_op jit(solution)/shard_map/deliver/pallas_call | solution.py:802

commit v3 on v2

--- a/solution.py
+++ b/solution.py
@@ -105,6 +105,8 @@
     back = (1, 0, 3, 2, 7, 6, 5, 4)
 
     def at(r, count=SUB):
+        if not isinstance(r, int):
+            return pl.ds(r, count)
         if r % SUB == 0:
             return slice(r, r + count)
         return pl.ds(zero + r, count)
@@ -194,8 +196,8 @@
         per = LANES // width
         chunk = lane // width
         for g in range(columns(len(targets), width)):
-            after = [got[0, column + g, r : r + SUB, :] for r in rows]
-            before = [got[1, column + g, r : r + SUB, :] for r in rows]
+            after = [got[0, column + g, at(r), :] for r in rows]
+            before = [got[1, column + g, at(r), :] for r in rows]
             for p, target in enumerate(targets[g * per : (g + 1) * per]):
                 for n, r in enumerate(rows):
                     both = jnp.where(chunk == p, after[n], before[n])
@@ -208,7 +210,7 @@
 
     def halo(ref, *index):
         def put(r, value):
-            ref[(*index, tiles, slice(r, r + SUB), slice(None))] = value
+            ref[(*index, tiles, at(r), slice(None))] = value
 
         return put
 
@@ -219,10 +221,10 @@
     near_columns = columns(len(field_layers) + len(inner), WIDE)
 
     def take_from(s, count):
-        return SUB if s == 0 else SUB + nj - count
+        return SUB + s * (nj - count)
 
     def put_to(s, count):
-        return SUB + nj if s == 0 else SUB - count
+        return SUB + nj - s * (nj + count)
 
     def pack_rows(ref, send, start, count, first, stop, unroll, sides=(0, 1)):
         @pl.loop(first, stop, unroll=unroll)
@@ -275,9 +277,6 @@
         @pl.when(jnp.logical_not(has[back[d]]))
         def _():
             ref[...] = jnp.zeros(ref.shape, f32)
-
-    def row_message(d, send, got, rows, number):
-        return (d, send.at[d, :, rows, :], got.at[d, :, rows, :], number)
 
     def lane_messages(send, got, number):
         out = []
@@ -290,11 +289,10 @@
                 )
         return out
 
-    wide_rows = [row_message(d, ja_send, ja_got, slice(0, second), 0) for d in (0, 1)]
-    thin_rows = [row_message(d, ja_send, ja_got, slice(second, total_rows), 1) for d in (0, 1)]
+    rows_a = [(d, ja_send.at[d], ja_got.at[d], 0) for d in (0, 1)]
     lanes_a = lane_messages(ka_send, ka_got, 0)
     surf = [(2 + s, v0.at[:, 0, s * (tiles - 1)], surf_got.at[s], 2) for s in (0, 1)]
-    rows_c = [row_message(d, jc_send, jc_got, slice(None), 3) for d in (0, 1)]
+    rows_c = [(d, jc_send.at[d], jc_got.at[d], 3) for d in (0, 1)]
     lanes_c = lane_messages(kc_send, kc_got, 3)
     def rec_copy(step):
         return pltpu.make_async_remote_copy(
@@ -310,26 +308,25 @@
     pack_rows(field, ja_send, 0, WIDE, 1, ni, 3)
     arrived(load_inv)
     pack_rows([inv], ja_send, inv_at, SWEEPS, 1, ni - 1, 2)
+    arrived(load_offset)
+    arrived(load_vol)
+    pack_rows(shape, ja_send, second, 1, 0, ni, 2)
     pl.semaphore_wait(barrier, greeted)
     for step in range(1, groups):
         rec_copy(step).start()
-    start(*wide_rows[0])
+    for message in rows_a:
+        start(*message)
     pack_lanes(
         [edge(v0, c, i) for c, i in field_layers] + [edge(inv, i) for i in inner],
         ka_send,
         0,
         WIDE,
     )
-    arrived(load_offset)
-    arrived(load_vol)
     pack_lanes([edge(sb, c, i) for c, i in shape_layers], ka_send, near_columns, 1)
-    for message in lanes_a[:2]:
-        start(*message)
-    pack_rows(shape, ja_send, second, 1, 0, ni, 2)
-    for message in (thin_rows[0], *lanes_a[2:4], wide_rows[1], thin_rows[1], *lanes_a[4:]):
+    for message in lanes_a:
         start(*message)
     rec_got[me] = rec_send[...]
-    for d, _, dst, _ in wide_rows + thin_rows + lanes_a + surf + rows_c + lanes_c:
+    for d, _, dst, _ in rows_a + lanes_a + surf + rows_c + lanes_c:
         clear_missing(d, dst)
 
     def in_pairs(first, stop):
@@ -389,13 +386,6 @@
     field_halos = [halo(v0, c, i) for c, i in field_layers] + [halo(inv, i) for i in inner]
     shape_halos = [halo(sb, c, i) for c, i in shape_layers]
 
-    for message in lanes_a[:2]:
-        received(*message)
-    unpack_lanes(field_halos, ka_got, 0, WIDE, tile_rows)
-    keep_layer(ni - 1, own)
-    for s in range(SWEEPS):
-        sweep_a(s, s + 2, ni - 1, tile_rows)
-
     def target_of(code):
         row = jnp.floor((code + 0.5) * (1.0 / nk))
         return row, code - row * nk
@@ -447,16 +437,62 @@
     for message in surf:
         start(*message)
 
+    for message in lanes_a[:2]:
+        received(*message)
+    unpack_lanes(field_halos, ka_got, 0, WIDE, tile_rows)
+    keep_layer(ni - 1, own)
+    for s in range(SWEEPS):
+        sweep_a(s, s + 2, ni - 1, tile_rows)
+
+    def either(s, values):
+        return ((s == 0) & values[0]) | ((s == 1) & values[1])
+
+    def side_copy(s, send, got, number):
+        return pltpu.make_async_remote_copy(
+            src_ref=send.at[s],
+            dst_ref=got.at[s],
+            send_sem=sem_halo.at[0, number, s],
+            recv_sem=sem_halo.at[1, number, s],
+            device_id=(me - 1 + 2 * s, my),
+            device_id_type=MESH,
+        )
+
+    def corner_copy(s, b):
+        d = 4 + 2 * s + b
+        return pltpu.make_async_remote_copy(
+            src_ref=ka_send.at[b, :, pl.ds(pl.multiple_of(s * (nj - SUB), SUB), SUB), :],
+            dst_ref=ka_got.at[b, :, pl.ds(corner_row(s), SUB), :],
+            send_sem=sem_halo.at[0, 0, d],
+            recv_sem=sem_halo.at[1, 0, d],
+            device_id=(me - 1 + 2 * s, my - 1 + 2 * b),
+            device_id_type=MESH,
+        )
+
+    def corner_row(s):
+        return pl.multiple_of((1 - s) * (SUB + nj), SUB)
+
+    def outer_row(s):
+        return low_row + (1 - s) * (high_row - low_row)
+
     def outer(s):
-        rows = (end, top)[s]
-        for message in (wide_rows[s], thin_rows[s], *lanes_a[2 + 2 * s : 4 + 2 * s]):
-            received(*message)
+        comes = either(s, (near[1], near[0]))
+
+        @pl.when(comes)
+        def _():
+            side_copy(s, ja_send, ja_got, 0).wait_recv()
+
+        for b in (0, 1):
+
+            @pl.when(comes & near[3 - b])
+            def _(b=b):
+                corner_copy(s, b).wait_recv()
+
         unpack_rows(field, ja_got, 0, WIDE, 1, ni, 3, (s,))
         unpack_rows([inv], ja_got, inv_at, SWEEPS, 1, ni - 1, 2, (s,))
-        unpack_lanes(field_halos, ka_got, 0, WIDE, (rows.start,))
+        unpack_lanes(field_halos, ka_got, 0, WIDE, (corner_row(s),))
         unpack_rows(shape, ja_got, second, 1, 0, ni, 2, (s,))
-        unpack_lanes(shape_halos, ka_got, near_columns, 1, (rows.start,))
-        keep_layer(ni - 1, rows)
+        unpack_lanes(shape_halos, ka_got, near_columns, 1, (corner_row(s),))
+        keep_layer(ni - 1, pl.ds(corner_row(s), SUB))
 
     def shape_rows(rows):
         for r in rows:
@@ -473,9 +509,11 @@
                     keep = cell & (i < ni - 1)
                     sb[3, i, t, at(r), :] = jnp.where(keep, sb[3, i, t, at(r), :], 0.0)
 
-    outer(0)
+    later = lax.rem(me, 2)
+    sooner = 1 - later
+    outer(sooner)
     for s in range(SWEEPS):
-        sweep_a(s, s + 2, ni - 1, (high_row,))
+        sweep_a(s, s + 2, ni - 1, (outer_row(sooner),))
 
     unpack_lanes(shape_halos, ka_got, near_columns, 1, tile_rows)
     for message in surf:
@@ -488,7 +526,7 @@
             )
     keep_layer(0, slice(0, all_rows))
     for s in range(SWEEPS):
-        sweep_a(s, 1, s + 2, tile_rows + [high_row])
+        sweep_a(s, 1, s + 2, tile_rows + [outer_row(sooner)])
 
     def cross(a, b):
         return (
@@ -550,20 +588,24 @@
 
     def send_flux(s):
         pack_rows(field, jc_send, 0, SWEEPS, 1, ni - 1, 2, (s,))
-        start(*rows_c[s])
+
+        @pl.when(either(s, near[:2]))
+        def _():
+            side_copy(s, jc_send, jc_got, 3).start()
 
     for message in surf:
         sent(*message)
-    shape_rows(shifted_rows[1:])
-    gradients([(tile_rows[0], False)] + [(r, True) for r in tile_rows[1:]])
-    send_flux(1)
-
-    outer(1)
+    count = len(tile_rows)
+    shape_rows([low_row + (1 - sooner) * SUB + n * SUB for n in range(count)])
+    gradients([((1 - sooner) * SUB + n * SUB, n > 0) for n in range(count)])
+    send_flux(later)
+
+    outer(later)
     for s in range(SWEEPS):
-        sweep_a(s, 1, ni - 1, (low_row,))
-    shape_rows(shifted_rows[:1])
-    gradients([(0, False), (tile_rows[0], True)])
-    send_flux(0)
+        sweep_a(s, 1, ni - 1, (outer_row(later),))
+    shape_rows([outer_row(later)])
+    gradients([((1 - later) * (nj - SUB) + n * SUB, n > 0) for n in range(2)])
+    send_flux(sooner)
     pack_lanes([edge(v0, c, i) for c, i in flux_layers], kc_send, 0, SWEEPS)
     for message in lanes_c:
         start(*message)
@@ -686,7 +728,7 @@
         weighted, onehot_s, (((1,), (1,)), ((), ())), preferred_element_type=f32
     )
     sens_o[...] = out[0:3] + out[3:6] + out[6:9]
-    for message in wide_rows + thin_rows + lanes_a + rows_c + lanes_c:
+    for message in rows_a + lanes_a + rows_c + lanes_c:
         sent(*message)
     for step in range(1, groups):
         reply_copy(step).wait_send()

time: 50.8 us -> 44.7 us (0.88)
  Pallas kernels: 50 us -> 43.7 us
    pallas_call x1, Pallas kernels: 47.6 us -> 41.4 us  [body(): pl.pallas_call(functools.partial(kernel, groups, slabs), out_shape=(pltpu...]
where the time goes in v3:
time: 44.7 us; the launch traced here: 44.4 us
  Pallas kernels  43.7 us (98%)
  between operations  0.64 us (1%)
    pallas_call x1, Pallas kernels, body(): pl.pallas_call(functools.partial(kernel, groups, slabs), out_shape=(pltpu...  41.4 us
    pallas_call x1, Pallas kernels, body(): pl.pallas_call(deliver, out_shape=(jax.ShapeDtypeStruct(offset.shape, f32...  2.36 us

profile of v3, /device:TPU:0, one launch (start us, length us, event | category | flops | bytes accessed | tf_op | source)
XLA Modules:
  0.0 44.4 jit_solution(14748918397030113324)
XLA Ops:
  0.6 41.4 %warp_adjoint.1 = (f32[3,16,3,48,128]{4,3,2,1,0:T(8,128)S(1)}, f32[3,16,2,48,128]{4,3,2,1,0:T(8,128)S(1)}, f32[3,512]{1,0:T(4,128)S(1)}) custom-call(s32[512]{0:T(512)} %struct_h.1, s32[512]{0:T(512)} %bitcast.1, s32[512]{0:T(512)} %node_h.1, f32[512]{0:T(512)} %weight_h.1, f32[3,512]{1,0:T(4,128)} %disp_h.1, f32[3,16,32,256]{3,2,1,0:T(8,128)} %offset_h.1, ...), custom_call_target="tpu_custom_call" | custom-call | tf_op jit(solution)/shard_map/warp_adjoint/pallas_call | solution.py:790
  42.0 2.4 %deliver.1 = (f32[3,16,32,256]{3,2,1,0:T(8,128)}, f32[3,16,32,256]{3,2,1,0:T(8,128)}, f32[3,512]{1,0:T(4,128)}) custom-call(f32[3,16,3,48,128]{4,3,2,1,0:T(8,128)S(1)} %get-tuple-element.6.warp, f32[3,16,2,48,128]{4,3,2,1,0:T(8,128)S(1)} %get-tuple-element.7.adj, f32[3,512]{1,0:T(4,128)S(1)} %get-tuple-element.8.sens), custom_call_target="tpu_custom_call" | custom-call | tf_op jit(solution)/shard_map/deliver/pallas_call | solution.py:844

commit v4 on v3

--- a/solution.py
+++ b/solution.py
@@ -173,24 +173,23 @@
     first_lane, last_lane, left_half = lane == 0, lane == LANES - 1, lane < LANES // 2
     tile_rows = [SUB + r * SUB for r in range(nj // SUB)]
 
-    def pack_lanes(sources, send, column, width):
+    def pack_lanes(sources, send, column, width, tiles_at):
         per = LANES // width
         chunk = lane // width
         chunk_last = lax.rem(lane + width, LANES) // width
         for g in range(columns(len(sources), width)):
-            first = [jnp.zeros((SUB, LANES), f32) for _ in tile_rows]
+            first = [jnp.zeros((SUB, LANES), f32) for _ in tiles_at]
             last = list(first)
             for p, source in enumerate(sources[g * per : (g + 1) * per]):
-                for n, r in enumerate(tile_rows):
+                for n, r in enumerate(tiles_at):
                     both = jnp.where(left_half, source(0, r), source(tiles - 1, r))
                     if p:
                         both = pltpu.roll(both, p * width, 1)
                     first[n] = jnp.where(chunk == p, both, first[n])
                     last[n] = jnp.where(chunk_last == p, both, last[n])
-            for n in range(len(tile_rows)):
-                rows = slice(n * SUB, (n + 1) * SUB)
-                send[0, column + g, rows, :] = first[n]
-                send[1, column + g, rows, :] = last[n]
+            for n, r in enumerate(tiles_at):
+                send[0, column + g, at(r - SUB), :] = first[n]
+                send[1, column + g, at(r - SUB), :] = last[n]
 
     def unpack_lanes(targets, got, column, width, rows):
         per = LANES // width
@@ -206,7 +205,7 @@
                     target(r, both)
 
     def edge(ref, *index):
-        return lambda t, r: ref[(*index, t, slice(r, r + SUB), slice(None))]
+        return lambda t, r: ref[(*index, t, at(r), slice(None))]
 
     def halo(ref, *index):
         def put(r, value):
@@ -293,7 +292,7 @@
     lanes_a = lane_messages(ka_send, ka_got, 0)
     surf = [(2 + s, v0.at[:, 0, s * (tiles - 1)], surf_got.at[s], 2) for s in (0, 1)]
     rows_c = [(d, jc_send.at[d], jc_got.at[d], 3) for d in (0, 1)]
-    lanes_c = lane_messages(kc_send, kc_got, 3)
+    lanes_c = lane_messages(kc_send, kc_got, 3)[2:]
     def rec_copy(step):
         return pltpu.make_async_remote_copy(
             src_ref=rec_send,
@@ -321,13 +320,16 @@
         ka_send,
         0,
         WIDE,
+        tile_rows,
     )
-    pack_lanes([edge(sb, c, i) for c, i in shape_layers], ka_send, near_columns, 1)
+    pack_lanes([edge(sb, c, i) for c, i in shape_layers], ka_send, near_columns, 1, tile_rows)
     for message in lanes_a:
         start(*message)
     rec_got[me] = rec_send[...]
     for d, _, dst, _ in rows_a + lanes_a + surf + rows_c + lanes_c:
         clear_missing(d, dst)
+    for s in (0, 1):
+        clear_missing(2 + s, kc_got.at[s, :, own, :])
 
     def in_pairs(first, stop):
         def run(step):
@@ -600,33 +602,62 @@
     gradients([((1 - sooner) * SUB + n * SUB, n > 0) for n in range(count)])
     send_flux(later)
 
+    def flux_lanes(number, at_row, rows):
+        at_row = pl.multiple_of(at_row, SUB)
+        return [
+            (
+                2 + s,
+                kc_send.at[s, :, pl.ds(at_row - SUB, rows), :],
+                kc_got.at[s, :, pl.ds(at_row, rows), :],
+                number,
+            )
+            for s in (0, 1)
+        ]
+
+    edges_c = [edge(v0, c, i) for c, i in flux_layers]
+    early_at, late_at = SUB + (1 - sooner) * SUB, SUB + sooner * (nj - SUB)
+    early_rows = [early_at + n * SUB for n in range(count - 1)]
+    early_lanes = flux_lanes(3, early_at, nj - SUB)
+    late_lanes = flux_lanes(4, late_at, SUB)
+    pack_lanes(edges_c, kc_send, 0, SWEEPS, early_rows)
+    for message in early_lanes:
+        start(*message)
+
     outer(later)
     for s in range(SWEEPS):
         sweep_a(s, 1, ni - 1, (outer_row(later),))
     shape_rows([outer_row(later)])
     gradients([((1 - later) * (nj - SUB) + n * SUB, n > 0) for n in range(2)])
     send_flux(sooner)
-    pack_lanes([edge(v0, c, i) for c, i in flux_layers], kc_send, 0, SWEEPS)
-    for message in lanes_c:
+    pack_lanes(edges_c, kc_send, 0, SWEEPS, [late_at])
+    for message in late_lanes + lanes_c:
         start(*message)
     for s in range(SWEEPS):
         for c in range(3):
             for i in (0, ni - 1):
                 level[s][c, i] = jnp.zeros(v0.shape[2:], f32)
 
+    sub = iota((SUB, LANES), 0)
+
     def sweep_c(s, first, stop, rows, adds):
         src = level[s]
         last = s == SWEEPS - 1
+        inside = [
+            None if add else (r + sub >= SUB + SWEEPS) & (r + sub < SUB + nj - SWEEPS)
+            for r, add in zip(rows, adds)
+        ]
 
         @in_pairs(first, stop)
         def _(i):
             for c in range(3):
-                for r, (low, high) in zip(rows, adds):
+                for r, add, keep in zip(rows, adds, inside):
+                    low, high = add or whole
                     x, change = changes(src, c, i, r, tiles if last else every)
                     for t, delta in enumerate(change):
                         if t < tiles:
                             to = at(r + low, high - low)
-                            adj[c, i, t, to, :] = adj[c, i, t, to, :] + delta[low:high]
+                            part = delta[low:high] if add else jnp.where(keep, delta, 0.0)
+                            adj[c, i, t, to, :] = adj[c, i, t, to, :] + part
                         if not last:
                             level[s + 1][c, i, t, at(r), :] = (
                                 x[t] + inv[i, t, at(r), :] * delta
@@ -634,18 +665,28 @@
 
     whole = (0, SUB)
     flux_halos = [halo(v0, c, i) for c, i in flux_layers]
-    for message in lanes_c[:2]:
+    for message in early_lanes:
         received(*message)
-    unpack_lanes(flux_halos, kc_got, 0, SWEEPS, tile_rows)
-    inner_adds = [whole] * len(tile_rows)
+    unpack_lanes(flux_halos, kc_got, 0, SWEEPS, early_rows)
+    inner_adds = [whole] * count
     inner_adds[0] = (SWEEPS, SUB)
     inner_adds[-1] = (0, SUB - SWEEPS)
-    for s in range(SWEEPS - 1):
+    from_side = lambda n, side: [SUB + side * (nj - n * SUB) + k * SUB for k in range(n)]
+    half = count // 2
+    sweep_c(0, 1, ni - 1, from_side(half, later), [None] * half)
+    sweep_c(1, 1, ni - 1, from_side(half - 1, later), [None] * (half - 1))
+    for message in late_lanes:
+        received(*message)
+    unpack_lanes(flux_halos, kc_got, 0, SWEEPS, [late_at])
+    sweep_c(0, 1, ni - 1, from_side(count - half, sooner), [None] * (count - half))
+    rest = count - half + 1
+    sweep_c(1, 1, ni - 1, from_side(rest, sooner), [None] * rest)
+    for s in range(2, SWEEPS - 1):
         sweep_c(s, 1, ni - 1, tile_rows, inner_adds)
     mid_rows = shifted_rows[1:-1]
     sweep_c(SWEEPS - 1, 1, ni - 1, mid_rows, [whole] * len(mid_rows))
 
-    for message in rows_c + lanes_c[2:]:
+    for message in rows_c + lanes_c:
         received(*message)
     unpack_rows(field, jc_got, 0, SWEEPS, 1, ni - 1, 2)
     unpack_lanes(flux_halos, kc_got, 0, SWEEPS, (0, SUB + nj))
@@ -728,7 +769,7 @@
         weighted, onehot_s, (((1,), (1,)), ((), ())), preferred_element_type=f32
     )
     sens_o[...] = out[0:3] + out[3:6] + out[6:9]
-    for message in rows_a + lanes_a + rows_c + lanes_c:
+    for message in rows_a + lanes_a + rows_c + early_lanes + late_lanes + lanes_c:
         sent(*message)
     for step in range(1, groups):
         reply_copy(step).wait_send()
@@ -817,7 +858,7 @@
             pltpu.SemaphoreType.DMA((5,)),
             pltpu.SemaphoreType.DMA((2, groups)),
             pltpu.SemaphoreType.DMA((2, groups)),
-            pltpu.SemaphoreType.DMA((2, 4, 8)),
+            pltpu.SemaphoreType.DMA((2, 5, 8)),
             pltpu.SemaphoreType.DMA((5, tiles)),
         ],
         compiler_params=pltpu.CompilerParams(

time: 44.7 us -> 44.7 us (level)
  no operation moved by 1% of the time
where the time goes in v4:
time: 44.7 us; the launch traced here: 44.5 us
  Pallas kernels  43.9 us (98%)
  between operations  0.64 us (1%)
    pallas_call x1, Pallas kernels, body(): pl.pallas_call(functools.partial(kernel, groups, slabs), out_shape=(pltpu...  41.5 us
    pallas_call x1, Pallas kernels, body(): pl.pallas_call(deliver, out_shape=(jax.ShapeDtypeStruct(offset.shape, f32...  2.36 us

profile of v4, /device:TPU:0, one launch (start us, length us, event | category | flops | bytes accessed | tf_op | source)
XLA Modules:
  0.0 44.5 jit_solution(8003774307917422458)
XLA Ops:
  0.6 41.5 %warp_adjoint.1 = (f32[3,16,3,48,128]{4,3,2,1,0:T(8,128)S(1)}, f32[3,16,2,48,128]{4,3,2,1,0:T(8,128)S(1)}, f32[3,512]{1,0:T(4,128)S(1)}) custom-call(s32[512]{0:T(512)} %struct_h.1, s32[512]{0:T(512)} %bitcast.1, s32[512]{0:T(512)} %node_h.1, f32[512]{0:T(512)} %weight_h.1, f32[3,512]{1,0:T(4,128)} %disp_h.1, f32[3,16,32,256]{3,2,1,0:T(8,128)} %offset_h.1, ...), custom_call_target="tpu_custom_call" | custom-call | tf_op jit(solution)/shard_map/warp_adjoint/pallas_call | solution.py:831
  42.2 2.4 %deliver.1 = (f32[3,16,32,256]{3,2,1,0:T(8,128)}, f32[3,16,32,256]{3,2,1,0:T(8,128)}, f32[3,512]{1,0:T(4,128)}) custom-call(f32[3,16,3,48,128]{4,3,2,1,0:T(8,128)S(1)} %get-tuple-element.6.warp, f32[3,16,2,48,128]{4,3,2,1,0:T(8,128)S(1)} %get-tuple-element.7.adj, f32[3,512]{1,0:T(4,128)S(1)} %get-tuple-element.8.sens), custom_call_target="tpu_custom_call" | custom-call | tf_op jit(solution)/shard_map/deliver/pallas_call | solution.py:885
